TPU v7x, 32 devices: a whole 2x2x4 slice. The times are simulated.
32 devices in a mesh: seq: 8 (over z, y), head: 4 (over x, core).
Axes of the slice: x: 2, y: 2, z: 4, core: 2. Of those that a mesh axis runs over, the one named last changes fastest.
Arguments:
- queries: bfloat16 [8, 1024, 128], P('head', 'seq')
- keys: bfloat16 [8, 1024, 128], P('head', 'seq')
- values: bfloat16 [8, 1024, 128], P('head', 'seq'), may hold values from -6 to 6
- grad_out: bfloat16 [8, 1024, 128], P('head', 'seq'), may hold values from -96 to 96
- rand_ids: int32 [8, 16, 3], P('head', 'seq'), may hold values from 0 to 15, as said below
- global_ids: int32 [2], replicated, may hold values from 0 to 15
Outputs:
- grad_queries: bfloat16 [8, 1024, 128], P('head', 'seq')
- grad_keys: bfloat16 [8, 1024, 128], P('head', 'seq')
- grad_values: bfloat16 [8, 1024, 128], P('head', 'seq')
Inputs may be any that keep to these rules, and one draw needn't show every extreme that they name: `rand_ids`: for each head and slot j there is one number M, 0 <= M < 8, such that every query block b names in slot j a block e * 2 + l with e = (b // 2) XOR M and 0 <= l < 2.
All inputs are finite; a program needn't handle non-finite values.
Results may differ from a plain program's by a relative error of at most 0.03.
Values may be sent and summed in bfloat16 or wider, within the bound.
No kernel may reach another device: no remote copies, remote signals or barrier semaphores. Data moves between devices by JAX's collectives and lax.ppermute only.
A program may use at most 64 MiB of HBM per device.

v0:
```python
import functools
import math

import jax
import jax.numpy as jnp
from jax import lax
from jax.experimental import pallas as pl
from jax.experimental.pallas import tpu as pltpu
from jax.sharding import PartitionSpec as P


GATHER_BYTES = 8 * 2**20
KERNEL_VMEM = 16 * 2**20
LOG2E = math.log2(math.e)
NEVER = -1e30
GROUP = 4
NT = (((1,), (1,)), ((), ()))


def pack_kernel(sizes, ids_hbm, gids_hbm, k_ref, v_ref, q_ref, g_ref, a_ref, b_ref, ids_ref, gids_ref, sems):
    heads, _, rows, _, block_rows, slots, _ = sizes
    blocks = rows // block_rows
    small = [
        pltpu.make_async_copy(ids_hbm, ids_ref, sems.at[0]),
        pltpu.make_async_copy(gids_hbm, gids_ref, sems.at[1]),
    ]
    copies = []
    for i, (src, dst, first) in enumerate(
        ((k_ref, a_ref, 0), (v_ref, a_ref, heads), (q_ref, b_ref, 0), (g_ref, b_ref, heads))
    ):
        for h in range(heads):
            copies.append(
                pltpu.make_async_copy(
                    src.at[h], dst.at[pl.ds((first + h) * rows, rows)], sems.at[2 + i * heads + h]
                )
            )
    for c in small + copies:
        c.start()
    head_rows = a_ref.shape[0] - 2 * heads * rows
    row = lax.broadcasted_iota(jnp.int32, (head_rows, rows), 0)
    lane = lax.broadcasted_iota(jnp.int32, (head_rows, rows), 1)
    me = lax.axis_index("seq")
    block = jnp.zeros_like(lane)
    for n in range(1, blocks):
        block = block + jnp.where(lane >= n * block_rows, 1, 0)
    tile = me * blocks + block
    for c in small:
        c.wait()
    for h in range(heads):
        for j in range(slots):
            ids = jnp.full_like(lane, ids_ref[h, 0, j])
            for n in range(1, blocks):
                ids = jnp.where(block == n, ids_ref[h, n, j], ids)
            tile = jnp.where(row == h * slots + j, ids, tile)
    for n in range(gids_ref.shape[0]):
        tile = jnp.where(row == heads * slots + 1 + n, gids_ref[n], tile)
    a_ref[2 * heads * rows :] = tile.astype(jnp.float32).astype(jnp.bfloat16)
    b_ref[2 * heads * rows :] = tile.astype(jnp.float32).astype(jnp.bfloat16)
    for c in copies:
        c.wait()


class Shards:
    def __init__(self, sizes, a_refs, b_refs):
        self.heads, self.count, self.rows, self.width, self.block_rows, self.slots, self.gids = sizes
        self.blocks = self.rows // self.block_rows
        self.a, self.b = a_refs, b_refs
        self.scale = 1.0 / math.sqrt(self.width)
        self.rate = self.scale * LOG2E
        self.key_heads = [self.head(x) for x in a_refs]
        self.query_heads = [self.head(x) for x in b_refs]

    def part(self, refs, index, group):
        found = [refs[s][index * self.rows : (index + 1) * self.rows] for s in group]
        return found[0] if len(found) == 1 else jnp.concatenate(found)

    def k(self, h, group):
        return self.part(self.a, h, group)

    def v(self, h, group):
        return self.part(self.a, self.heads + h, group)

    def q(self, h, group):
        return self.part(self.b, h, group)

    def g(self, h, group):
        return self.part(self.b, self.heads + h, group)

    def key_ids(self, group):
        height = len(group) * self.blocks
        row = lax.broadcasted_iota(jnp.int32, (height, self.rows), 0).astype(jnp.float32)
        base = self.heads * self.slots
        nk = jnp.zeros((height, self.rows), jnp.float32)
        for i, s in enumerate(group):
            first = self.key_heads[s][base : base + 1, 0:1] - i * self.blocks
            nk = jnp.where(row >= i * self.blocks, row + first, nk)
        seen = jnp.zeros((height, self.rows), jnp.float32)
        for n in range(self.gids):
            gid = self.key_heads[group[0]][base + 1 + n : base + 2 + n]
            seen = seen + jnp.where(nk == gid, 1.0, 0.0)
        return nk, seen

    def head(self, ref):
        return ref[2 * self.heads * self.rows :].astype(jnp.float32)

    def bias(self, keys, group):
        nk, seen = keys
        out = []
        for h in range(self.heads):
            cols = []
            for s in group:
                head = self.query_heads[s]
                nq = head[self.heads * self.slots :][:1]
                count = seen + jnp.where(jnp.abs(nk - nq) <= 1.0, 1.0, 0.0)
                for j in range(self.slots):
                    r = h * self.slots + j
                    count = count + jnp.where(nk == head[r : r + 1], 1.0, 0.0)
                cols.append(jnp.where(count > 0.5, jnp.log2(jnp.maximum(count, 1.0)), NEVER))
            out.append(cols[0] if len(cols) == 1 else jnp.concatenate(cols, axis=1))
        return out

    def scores(self, h, keys, queries):
        return (
            lax.dot_general(self.k(h, keys), self.q(h, queries), NT, preferred_element_type=jnp.float32),
            lax.dot_general(self.v(h, keys), self.g(h, queries), NT, preferred_element_type=jnp.float32),
        )

    def stats(self, scored, bias, keep):
        s, dp = scored
        lanes = s.shape[1]
        steps = self.block_rows // 8
        top = None
        for kb in range(bias.shape[0]):
            x = s[kb * self.block_rows : (kb + 1) * self.block_rows] * self.rate + bias[kb : kb + 1]
            x = jnp.max(x.reshape(steps, 8, lanes), axis=0)
            top = x if top is None else jnp.maximum(top, x)
        top = jnp.maximum(jnp.max(top, axis=0, keepdims=True), 0.5 * NEVER)
        acc_l = acc_d = None
        for kb in range(bias.shape[0]):
            cut = slice(kb * self.block_rows, (kb + 1) * self.block_rows)
            e = jnp.exp2(s[cut] * self.rate + (bias[kb : kb + 1] - top))
            keep(kb, cut, e, dp[cut])
            d = jnp.sum((e * dp[cut]).reshape(steps, 8, lanes), axis=0)
            e = jnp.sum(e.reshape(steps, 8, lanes), axis=0)
            acc_l = e if acc_l is None else acc_l + e
            acc_d = d if acc_d is None else acc_d + d
        return top, jnp.sum(acc_l, axis=0, keepdims=True), jnp.sum(acc_d, axis=0, keepdims=True)


def stats_kernel(sizes, widths, *refs):
    n_keys, n_queries = widths
    a_refs, b_refs = refs[:n_keys], refs[n_keys : n_keys + n_queries]
    stat, e_ref, dp_ref = refs[n_keys + n_queries :]
    sh = Shards(sizes, a_refs, b_refs)
    keys, queries = list(range(n_keys)), list(range(n_queries))
    bias = sh.bias(sh.key_ids(keys), queries)
    scored = [sh.scores(h, keys, queries) for h in range(sh.heads)]
    for h in range(sh.heads):

        def keep(kb, cut, e, dp):
            e_ref[h, cut] = e
            dp_ref[h, cut] = dp

        for i, x in enumerate(sh.stats(scored[h], bias[h], keep)):
            stat[3 * h + i : 3 * h + i + 1] = x


def partner_kernel(sizes, widths, *refs):
    heads, rows = sizes[0], sizes[2]
    n_keys, n_queries = widths
    a_refs, (stat, e_ref, dp_ref) = refs[:n_keys], refs[n_keys : n_keys + 3]
    outs = refs[n_keys + 3 :]
    sh = Shards(sizes, a_refs, ())
    tn = (((0,), (0,)), ((), ()))
    for s in range(1, n_queries):
        lanes = slice(s * rows, (s + 1) * rows)
        for h in range(heads):
            k = sh.k(h, list(range(n_keys)))
            local = local_dot(stat, h, lanes)
            low, e_low = [], []
            for r in range(0, n_keys * rows, sh.block_rows):
                e = e_ref[h, r : r + sh.block_rows, lanes]
                e_low.append(e.astype(jnp.bfloat16))
                low.append((e * (dp_ref[h, r : r + sh.block_rows, lanes] - local)).astype(jnp.bfloat16))
            for i, x in enumerate((low, e_low)):
                x = lax.dot_general(jnp.concatenate(x), k, tn, preferred_element_type=jnp.float32)
                outs[s - 1][(i * heads + h) * rows : (i * heads + h + 1) * rows] = x.astype(outs[s - 1].dtype)


def local_dot(stat, h, lanes):
    total = stat[3 * h + 1 : 3 * h + 2, lanes]
    return stat[3 * h + 2 : 3 * h + 3, lanes] / jnp.where(total > 0.0, total, 1.0)


def whole_stats(stats, rows, h, s):
    holders = range(len(stats))

    def part(i, p):
        return stats[p][3 * h + i : 3 * h + i + 1, (s ^ p) * rows : ((s ^ p) + 1) * rows]

    top = functools.reduce(jnp.maximum, [part(0, p) for p in holders])
    scales = [jnp.exp2(part(0, p) - top) for p in holders]
    total = sum(part(1, p) * w for p, w in zip(holders, scales))
    weighted = sum(part(2, p) * w for p, w in zip(holders, scales))
    return top + jnp.log2(total), weighted / total


def grads_kernel(sizes, widths, *refs):
    heads, rows = sizes[0], sizes[2]
    n_keys, n_queries = widths
    b_refs = refs[:n_queries]
    stats, (e_ref, dp_ref) = refs[n_queries : 2 * n_queries], refs[2 * n_queries : 2 * n_queries + 2]
    kv_out = refs[2 * n_queries + 2 :]
    sh = Shards(sizes, (), b_refs)
    queries = list(range(n_queries))
    for h in range(heads):
        whole = [whole_stats(stats, rows, h, s) for s in queries]
        shift, dots = (jnp.concatenate([x[i] for x in whole], axis=1) for i in range(2))
        w = jnp.exp2(stats[0][3 * h : 3 * h + 1] - shift)
        p_low, ds_low = [], []
        for r in range(0, n_keys * rows, sh.block_rows):
            cut = slice(r, r + sh.block_rows)
            p = e_ref[h, cut] * w
            p_low.append(p.astype(jnp.bfloat16))
            ds_low.append((p * (dp_ref[h, cut] - dots)).astype(jnp.bfloat16))
        dk = jnp.dot(jnp.concatenate(ds_low), sh.q(h, queries), preferred_element_type=jnp.float32) * sh.scale
        dv = jnp.dot(jnp.concatenate(p_low), sh.g(h, queries), preferred_element_type=jnp.float32)
        for m in range(n_keys):
            cut = slice(m * rows, (m + 1) * rows)
            kv_out[m][h * rows : (h + 1) * rows] = dk[cut].astype(kv_out[m].dtype)
            kv_out[m][(heads + h) * rows : (heads + h + 1) * rows] = dv[cut].astype(kv_out[m].dtype)


def queries_kernel(sizes, widths, *refs):
    heads, rows = sizes[0], sizes[2]
    n_keys, n_queries = widths
    a_refs, refs = refs[:n_keys], refs[n_keys:]
    stats, (e_ref, dp_ref), refs = refs[:n_queries], refs[n_queries : n_queries + 2], refs[n_queries + 2 :]
    sums, out = refs[: n_queries - 1], refs[-1]
    sh = Shards(sizes, a_refs, ())
    for h in range(heads):
        shift, dots = whole_stats(stats, rows, h, 0)
        w = jnp.exp2(stats[0][3 * h : 3 * h + 1, 0:rows] - shift)
        low = []
        for r in range(0, n_keys * rows, sh.block_rows):
            cut = slice(r, r + sh.block_rows)
            low.append(((e_ref[h, cut, 0:rows] * w) * (dp_ref[h, cut, 0:rows] - dots)).astype(jnp.bfloat16))
        dq = lax.dot_general(
            jnp.concatenate(low), sh.k(h, list(range(n_keys))), (((0,), (0,)), ((), ())),
            preferred_element_type=jnp.float32,
        )
        for p in range(1, n_queries):
            lanes = slice(p * rows, (p + 1) * rows)
            w = jnp.exp2(stats[p][3 * h : 3 * h + 1, lanes] - shift)
            moved = w * (local_dot(stats[p], h, lanes) - dots)
            w, moved = (jnp.broadcast_to(x, (rows, rows)).T for x in (w, moved))
            first = sums[p - 1][h * rows : (h + 1) * rows].astype(jnp.float32)
            second = sums[p - 1][(heads + h) * rows : (heads + h + 1) * rows].astype(jnp.float32)
            dq = dq + (first * w + second * moved)
        out[h] = (dq * sh.scale).astype(out.dtype)


def sum_kernel(sizes, n_keys, *refs):
    heads, rows = sizes[0], sizes[2]
    parts, outs, bufs, sems = refs[:n_keys], refs[n_keys : n_keys + 2], refs[n_keys + 2 : -1], refs[-1]
    copies = []
    for i in range(2):
        for h in range(heads):
            cut = slice((i * heads + h) * rows, (i * heads + h + 1) * rows)
            total = sum(p[cut].astype(jnp.float32) for p in parts)
            bufs[i][h] = total.astype(bufs[i].dtype)
        copies.append(pltpu.make_async_copy(bufs[i], outs[i], sems.at[i]))
        copies[-1].start()
    for c in copies:
        c.wait()


def near(arrays):
    return [pltpu.with_memory_space_constraint(x, pltpu.VMEM) for x in arrays]


def exchanged(value, mask):
    return lax.ppermute(value, "seq", [(i, i ^ mask) for i in range(lax.axis_size("seq"))])


def key_moves(n_keys):
    direct = [m for m in range(n_keys - 1, 0, -1) if m & (m - 1) == 0]
    relayed = [m for m in range(1, n_keys) if m not in direct]
    return [(m, m) for m in direct], [(m, m & -m) for m in relayed]


def gathered(queries, keys, values, grad_out, rand_ids, global_ids):
    heads, rows, width = queries.shape
    blocks, slots = rand_ids.shape[1:]
    count = lax.axis_size("seq")
    n_keys = min(GROUP, count)
    n_queries = count // n_keys
    widths = (n_keys, n_queries)
    sizes = (heads, count, rows, width, rows // blocks, slots, global_ids.shape[0])
    head_rows = -(-(heads * slots + 1 + global_ids.shape[0]) // 16) * 16
    vmem = pl.BlockSpec(memory_space=pltpu.VMEM)
    anyspace = pl.BlockSpec(memory_space=pl.ANY)
    params = pltpu.CompilerParams(vmem_limit_bytes=KERNEL_VMEM)
    a, b = pl.pallas_call(
        functools.partial(pack_kernel, sizes),
        out_shape=(pltpu.VMEM((2 * heads * rows + head_rows, width), queries.dtype),) * 2,
        in_specs=[anyspace] * 6,
        out_specs=(vmem, vmem),
        scratch_shapes=[
            pltpu.SMEM(rand_ids.shape, jnp.int32),
            pltpu.SMEM(global_ids.shape, jnp.int32),
            pltpu.SemaphoreType.DMA((2 + 4 * heads,)),
        ],
    )(rand_ids, global_ids, keys, values, queries, grad_out)

    b_all = [b] + [exchanged(b, s * n_keys) for s in range(1, n_queries)]
    a_all = {0: a}
    for moves in key_moves(n_keys):
        for m, last in moves:
            a_all[m] = exchanged(a_all[m - last], last)
    a_all = [a_all[m] for m in range(n_keys)]
    lanes = n_queries * rows
    stat_rows = -(-3 * heads // 8) * 8
    stat, e, dp = pl.pallas_call(
        functools.partial(stats_kernel, sizes, widths),
        out_shape=(pltpu.VMEM((stat_rows, lanes), jnp.float32),)
        + (pltpu.VMEM((heads, n_keys * rows, lanes), jnp.float32),) * 2,
        compiler_params=params,
        in_specs=[vmem] * count_of(widths),
        out_specs=(vmem,) * 3,
    )(*near(a_all), *near(b_all))
    stats = [stat] + [exchanged(stat, s * n_keys) for s in range(1, n_queries)]
    sums = pl.pallas_call(
        functools.partial(partner_kernel, sizes, widths),
        out_shape=(pltpu.VMEM((2 * heads * rows, width), queries.dtype),) * (n_queries - 1),
        compiler_params=params,
        in_specs=[vmem] * (n_keys + 3),
        out_specs=(vmem,) * (n_queries - 1),
    )(*near(a_all), *near([stat, e, dp]))
    sums = [exchanged(x, s * n_keys) for s, x in zip(range(1, n_queries), sums)]
    shapes = [pltpu.VMEM((2 * heads * rows, width), jnp.float32)]
    shapes += [pltpu.VMEM((2 * heads * rows, width), queries.dtype)] * (n_keys - 1)
    parts = pl.pallas_call(
        functools.partial(grads_kernel, sizes, widths),
        out_shape=tuple(shapes),
        compiler_params=params,
        in_specs=[vmem] * (2 * n_queries + 2),
        out_specs=(vmem,) * len(shapes),
    )(*near(b_all), *near(stats), *near([e, dp]))
    parts = [parts[0]] + [exchanged(parts[m], m) for m in range(1, n_keys)]
    out = jax.ShapeDtypeStruct(queries.shape, queries.dtype)
    grad_queries = pl.pallas_call(
        functools.partial(queries_kernel, sizes, widths),
        out_shape=out,
        compiler_params=params,
        in_specs=[vmem] * (n_keys + 2 * n_queries + 1),
        out_specs=vmem,
    )(*near(a_all), *near(stats), *near([e, dp]), *near(sums))
    buf = pltpu.VMEM(queries.shape, queries.dtype)
    grad_keys, grad_values = pl.pallas_call(
        functools.partial(sum_kernel, sizes, n_keys),
        out_shape=(out, out),
        compiler_params=params,
        in_specs=[vmem] * n_keys,
        out_specs=(anyspace,) * 2,
        scratch_shapes=[buf, buf, pltpu.SemaphoreType.DMA((2,))],
    )(*near(parts))
    return grad_queries, grad_keys, grad_values


def count_of(widths):
    return widths[0] + widths[1]


def with_halo(value, sides, width):
    for axis, dim in sides:
        peers, length = (lax.axis_size(axis), value.shape[dim])
        up = [(i, (i + 1) % peers) for i in range(peers - 1)]
        down = [(j, i) for i, j in up]
        last = lax.slice_in_dim(value, length - width, length, axis=dim)
        initial = lax.slice_in_dim(value, 0, width, axis=dim)
        before = lax.ppermute(last, axis, up)
        after = lax.ppermute(initial, axis, down)
        value = jnp.concatenate([before, value, after], axis=dim)
    return value


def swapped(value, axis, distance):
    mask = 2**distance
    pairs = [(source, source ^ mask) for source in range(lax.axis_size(axis))]
    return lax.ppermute(value, axis, pairs)


def section_list(section_count):
    return list(range(section_count))


def routed(queries, keys, values, grad_out, rand_ids, global_ids):
    head_count, row_count, head_width = queries.shape
    block_count = rand_ids.shape[1]
    slot_count = rand_ids.shape[2]
    block_rows = row_count // block_count
    global_count = global_ids.shape[0]
    slot_total = 3 + global_count + slot_count
    device = lax.axis_index("seq")
    seq_count = lax.axis_size("seq")
    sections = section_list(seq_count.bit_length() - 1)
    score_scale = 1.0 / math.sqrt(head_width)
    key_vals = jnp.stack([keys, values])
    padded = with_halo(key_vals, (("seq", 2),), block_rows)
    padded_blocks = padded.reshape(2, head_count, block_count + 2, block_rows, head_width)
    window = jnp.stack(
        [
            padded_blocks[:, :, 0:block_count],
            padded_blocks[:, :, 1 : block_count + 1],
            padded_blocks[:, :, 2 : block_count + 2],
        ],
        3,
    )
    key_blocks = key_vals.reshape(2, head_count, block_count, block_rows, head_width)
    global_local = global_ids % block_count
    global_owner = global_ids // block_count
    owned = (global_owner == device).astype(jnp.float32)
    picked = jnp.take(key_blocks, global_local, axis=2).astype(jnp.float32)
    global_sum = lax.psum(picked * owned[None, None, :, None, None], "seq")
    global_kv = global_sum.astype(jnp.bfloat16)
    global_keys = jnp.broadcast_to(
        global_kv[:, :, None], (2, head_count, block_count, global_count, block_rows, head_width)
    )
    xor_masks = jnp.bitwise_xor(rand_ids[:, 0, :] // block_count, device)
    pieces = []
    for slot_index in range(slot_count):
        moving = key_vals
        for bit_index in sections:
            arrived = swapped(moving, "seq", bit_index)
            flag_now = jnp.right_shift(xor_masks[:, slot_index], bit_index) & 1 == 1
            moving = jnp.where(flag_now[None, :, None, None], arrived, moving)
        pieces.append(moving)
    routed = jnp.stack(pieces)
    routed_blocks = routed.reshape(slot_count, 2, head_count, block_count, block_rows, head_width)
    random_local = rand_ids % block_count
    local_onehot = (random_local[..., None] == jnp.arange(block_count, dtype=jnp.int32)).astype(
        jnp.bfloat16
    )
    random_keys = jnp.einsum(
        "hqjl,jchlbd->chqjbd", local_onehot, routed_blocks, preferred_element_type=jnp.float32
    ).astype(jnp.bfloat16)
    all_keys = jnp.concatenate([window, global_keys, random_keys], axis=3)
    key_list = all_keys[0].reshape(head_count, block_count, slot_total * block_rows, head_width)
    value_list = all_keys[1].reshape(head_count, block_count, slot_total * block_rows, head_width)
    block_range = jnp.arange(block_count, dtype=jnp.int32)
    left_valid = jnp.logical_not((block_range == 0) & (device == 0))
    right_valid = jnp.logical_not((block_range == block_count - 1) & (device == seq_count - 1))
    valid = jnp.concatenate(
        [
            left_valid[:, None],
            jnp.ones((block_count, 1), bool),
            right_valid[:, None],
            jnp.ones((block_count, global_count + slot_count), bool),
        ],
        1,
    )
    mask = jnp.repeat(valid, block_rows, axis=1)[None, :, None, :]
    query_blocks = queries.reshape(head_count, block_count, block_rows, head_width)
    grad_blocks = grad_out.reshape(head_count, block_count, block_rows, head_width)
    scores = (
        jnp.einsum("hnqd,hnkd->hnqk", query_blocks, key_list, preferred_element_type=jnp.float32)
        * score_scale
    )
    row_max = jnp.max(jnp.where(mask, scores, -1e30), -1)
    total = jnp.sum(jnp.where(mask, jnp.exp(scores - row_max[..., None]), 0.0), -1)
    log_total = row_max + jnp.log(total)
    probs = jnp.where(mask, jnp.exp(scores - log_total[..., None]), 0.0)
    probs_low = probs.astype(jnp.bfloat16)
    output = jnp.einsum(
        "hnqk,hnkd->hnqd", probs_low, value_list, preferred_element_type=jnp.float32
    )
    row_dot = jnp.sum(grad_blocks.astype(jnp.float32) * output, -1)
    grad_probs = jnp.einsum(
        "hnqd,hnkd->hnqk", grad_blocks, value_list, preferred_element_type=jnp.float32
    )
    scores_low = (probs * (grad_probs - row_dot[..., None])).astype(jnp.bfloat16)
    grad_query = score_scale * jnp.einsum(
        "hnqk,hnkd->hnqd", scores_low, key_list, preferred_element_type=jnp.float32
    )
    key_terms = score_scale * jnp.einsum(
        "hnqk,hnqd->hnkd", scores_low, query_blocks, preferred_element_type=jnp.float32
    )
    value_terms = jnp.einsum(
        "hnqk,hnqd->hnkd", probs_low, grad_blocks, preferred_element_type=jnp.float32
    )
    grads = jnp.stack([key_terms, value_terms]).reshape(
        2, head_count, block_count, slot_total, block_rows, head_width
    )
    no_pad = (0, 0)
    frame_sum = jnp.pad(grads[:, :, :, 0], (no_pad, no_pad, (0, 2), no_pad, no_pad))
    frame_sum = frame_sum + jnp.pad(grads[:, :, :, 1], (no_pad, no_pad, (1, 1), no_pad, no_pad))
    frame_sum = frame_sum + jnp.pad(grads[:, :, :, 2], (no_pad, no_pad, (2, 0), no_pad, no_pad))
    own_grads = frame_sum[:, :, 1 : block_count + 1]
    rim_parts = jnp.concatenate([frame_sum[:, :, 0], frame_sum[:, :, block_count + 1]], axis=2)
    rim_back = with_halo(rim_parts.astype(jnp.bfloat16), (("seq", 2),), block_rows).astype(
        rim_parts.dtype
    )
    own_grads = own_grads.at[:, :, 0].add(rim_back[:, :, 0:block_rows])
    own_grads = own_grads.at[:, :, block_count - 1].add(
        rim_back[:, :, 3 * block_rows : 4 * block_rows]
    )
    global_part = jnp.sum(grads[:, :, :, 3 : 3 + global_count], axis=2)
    global_total = lax.psum(global_part, "seq")
    global_onehot = (
        (global_local[:, None] == block_range[None, :]) & (global_owner == device)[:, None]
    ).astype(jnp.float32)
    own_grads = own_grads + jnp.einsum(
        "gn,chgbd->chnbd", global_onehot, global_total, precision=lax.Precision.HIGHEST
    )
    random_part = grads[:, :, :, 3 + global_count :]
    local_float = (random_local[..., None] == block_range).astype(jnp.float32)
    send_back = jnp.einsum(
        "hqjl,chqjbd->jchlbd", local_float, random_part, precision=lax.Precision.HIGHEST
    )
    send_back = send_back.astype(jnp.bfloat16).reshape(
        slot_count, 2, head_count, row_count, head_width
    )
    pieces = []
    for slot_index in range(slot_count):
        moving = send_back[slot_index]
        for bit_index in sections:
            arrived = swapped(moving, "seq", bit_index)
            flag_now = jnp.right_shift(xor_masks[:, slot_index], bit_index) & 1 == 1
            moving = jnp.where(flag_now[None, :, None, None], arrived, moving)
        pieces.append(moving)
    returned = jnp.stack(pieces)
    returned_sum = jnp.sum(returned.astype(jnp.float32), axis=0).reshape(
        2, head_count, block_count, block_rows, head_width
    )
    own_grads = own_grads + returned_sum
    grad_queries = grad_query.reshape(head_count, row_count, head_width).astype(jnp.bfloat16)
    grad_keys = own_grads[0].reshape(head_count, row_count, head_width).astype(jnp.bfloat16)
    grad_values = own_grads[1].reshape(head_count, row_count, head_width).astype(jnp.bfloat16)
    return (grad_queries, grad_keys, grad_values)


def on_device(queries, keys, values, grad_out, rand_ids, global_ids):
    count = lax.axis_size("seq")
    rows, width = queries.shape[1:]
    gathered_bytes = 4 * count * queries.size * queries.dtype.itemsize
    if gathered_bytes <= GATHER_BYTES and count & (count - 1) == 0 and rows == width:
        return gathered(queries, keys, values, grad_out, rand_ids, global_ids)
    return routed(queries, keys, values, grad_out, rand_ids, global_ids)


def solution(mesh):
    in_specs = (
        P("head", "seq", None),
        P("head", "seq", None),
        P("head", "seq", None),
        P("head", "seq", None),
        P("head", "seq", None),
        P(),
    )
    out_specs = (P("head", "seq", None), P("head", "seq", None), P("head", "seq", None))
    return jax.shard_map(
        on_device, mesh=mesh, in_specs=in_specs, out_specs=out_specs, check_vma=False
    )
```

profile of v0, /device:TPU:0, one launch (start us, length us, event | category | flops | bytes accessed | tf_op | source)
XLA Modules:
  0.0 30.1 jit_solution(1276456034012442277)
XLA Ops:
  0.6 1.0 %shard_map.85 = (bf16[528,128]{1,0:T(8,128)(2,1)S(1)}, bf16[528,128]{1,0:T(8,128)(2,1)S(1)}) custom-call(s32[2,2,3]{2,1,0:T(2,128)} %ids_hbm.1, s32[2]{0:T(128)} %gids_hbm.1, bf16[2,128,128]{2,1,0:T(8,128)(2,1)} %k_ref.1, bf16[2,128,128]{2,1,0:T(8,128)(2,1)} %v_ref.1, bf16[2,128,128]{2,1,0:T(8,128)(2,1)} %q_ref.1, bf16[2,128,128]{2,1,0:T(8,128)(2,1)} %g_ref.1), custom_call_target="tpu_custom_call" | custom-call | tf_op jit(solution)/shard_map/pallas_call | solution.py:304
  1.6 3.1 %collective-permute-start.1 = (bf16[528,128]{1,0:T(8,128)(2,1)S(1)}, bf16[528,128]{1,0:T(8,128)(2,1)S(1)}, u32[]{:S(2)}, u32[]{:S(2)}) collective-permute-start(bf16[528,128]{1,0:T(8,128)(2,1)S(1)} %get-tuple-element.14.refs_0_), channel_id=1, source_target_pairs={{0,8},{4,12},{8,0},{12,4},{16,24},{20,28},{24,16},{28,20},{1,9},{5... | collective-permute-start | bytes 405512 | tf_op jit(solution)/shard_map/ppermute | solution.py:283
  4.7 1.5 %collective-permute-start = (bf16[528,128]{1,0:T(8,128)(2,1)S(1)}, bf16[528,128]{1,0:T(8,128)(2,1)S(1)}, u32[]{:S(2)}, u32[]{:S(2)}) collective-permute-start(bf16[528,128]{1,0:T(8,128)(2,1)S(1)} %get-tuple-element.14.refs_0_), channel_id=1, source_target_pairs={{0,4},{4,0},{8,12},{12,8},{16,20},{20,16},{24,28},{28,24},{1,5},{5... | collective-permute-start | bytes 405512 | tf_op jit(solution)/shard_map/ppermute | solution.py:283
  6.2 2.6 %collective-permute-start.3 = (bf16[528,128]{1,0:T(8,128)(2,1)S(1)}, bf16[528,128]{1,0:T(8,128)(2,1)S(1)}, u32[]{:S(2)}, u32[]{:S(2)}) collective-permute-start(bf16[528,128]{1,0:T(8,128)(2,1)S(1)} %get-tuple-element.15.refs_4_.refs_0_), channel_id=1, source_target_pairs={{0,16},{4,20},{8,24},{12,28},{16,0},{20,4},{24,8},{28,12},{1,17},{... | collective-permute-start | bytes 405512 | tf_op jit(solution)/shard_map/ppermute | solution.py:283
  8.8 0.0 collective-permute-done.1.refs_2_
  8.8 2.8 %collective-permute-start.2 = (bf16[528,128]{1,0:T(8,128)(2,1)S(1)}, bf16[528,128]{1,0:T(8,128)(2,1)S(1)}, u32[]{:S(2)}, u32[]{:S(2)}) collective-permute-start(bf16[528,128]{1,0:T(8,128)(2,1)S(1)} %collective-permute-done.1.refs_2_), channel_id=1, source_target_pairs={{0,4},{4,0},{8,12},{12,8},{16,20},{20,16},{24,28},{28,24},{1,5},{5... | collective-permute-start | bytes 405512 | tf_op jit(solution)/shard_map/ppermute | solution.py:283
  11.7 3.1 %collective-permute-done.3.refs_5_.refs_1_ = bf16[528,128]{1,0:T(8,128)(2,1)S(1)} collective-permute-done((bf16[528,128]{1,0:T(8,128)(2,1)S(1)}, bf16[528,128]{1,0:T(8,128)(2,1)S(1)}, u32[]{:S(2)}, u32[]{:S(2)}) %collective-permute-start.3) | collective-permute-done | bytes 135200 | tf_op jit(solution)/shard_map/ppermute | solution.py:283
  14.8 0.0 collective-permute-done.refs_1_
  14.8 0.0 collective-permute-done.2.refs_3_
  14.8 0.6 %shard_map.86 = (f32[8,256]{1,0:T(8,128)S(1)}, f32[2,512,256]{2,1,0:T(8,128)S(1)}, f32[2,512,256]{2,1,0:T(8,128)S(1)}) custom-call(bf16[528,128]{1,0:T(8,128)(2,1)S(1)} %get-tuple-element.14.refs_0_, bf16[528,128]{1,0:T(8,128)(2,1)S(1)} %collective-permute-done.refs_1_, bf16[528,128]{1,0:T(8,128)(2,1)S(1)} %collective-permute-done.1.refs_2_, ...), custom_call_target="tpu_custom_call" | custom-call | tf_op jit(solution)/shard_map/pallas_call | solution.py:324
  15.4 2.5 %collective-permute-start.4 = (f32[8,256]{1,0:T(8,128)S(1)}, f32[8,256]{1,0:T(8,128)S(1)}, u32[]{:S(2)}, u32[]{:S(2)}) collective-permute-start(f32[8,256]{1,0:T(8,128)S(1)} %get-tuple-element.16.refs_4_.refs_2_), channel_id=1, source_target_pairs={{0,16},{4,20},{8,24},{12,28},{16,0},{20,4},{24,8},{28,12},{1,17},{... | collective-permute-start | bytes 24584 | tf_op jit(solution)/shard_map/ppermute | solution.py:283
  17.9 0.4 %shard_map.87 = bf16[512,128]{1,0:T(8,128)(2,1)S(1)} custom-call(bf16[528,128]{1,0:T(8,128)(2,1)S(1)} %get-tuple-element.14.refs_0_, bf16[528,128]{1,0:T(8,128)(2,1)S(1)} %collective-permute-done.refs_1_, bf16[528,128]{1,0:T(8,128)(2,1)S(1)} %collective-permute-done.1.refs_2_, bf16[528,128]{1,0:T(8,128)(2,1)S(1)} %collective-permute-done.2.refs_3_, ...), custom_call_target="tpu_custom_call" | custom-call | tf_op jit(solution)/shard_map/pallas_call | solution.py:333
  18.3 0.6 %collective-permute-start.5 = (bf16[512,128]{1,0:T(8,128)(2,1)S(1)}, bf16[512,128]{1,0:T(8,128)(2,1)S(1)}, u32[]{:S(2)}, u32[]{:S(2)}) collective-permute-start(bf16[512,128]{1,0:T(8,128)(2,1)S(1)} %shard_map.87), channel_id=1, source_target_pairs={{0,16},{4,20},{8,24},{12,28},{16,0},{20,4},{24,8},{28,12},{1,17},{... | collective-permute-start | bytes 393224 | tf_op jit(solution)/shard_map/ppermute | solution.py:283
  18.9 1.2 %collective-permute-done.4.refs_5_.refs_3_ = f32[8,256]{1,0:T(8,128)S(1)} collective-permute-done((f32[8,256]{1,0:T(8,128)S(1)}, f32[8,256]{1,0:T(8,128)S(1)}, u32[]{:S(2)}, u32[]{:S(2)}) %collective-permute-start.4) | collective-permute-done | bytes 8224 | tf_op jit(solution)/shard_map/ppermute | solution.py:283
  20.1 0.5 %shard_map.89 = (f32[512,128]{1,0:T(8,128)S(1)}, bf16[512,128]{1,0:T(8,128)(2,1)S(1)}, bf16[512,128]{1,0:T(8,128)(2,1)S(1)}, bf16[512,128]{1,0:T(8,128)(2,1)S(1)}) custom-call(bf16[528,128]{1,0:T(8,128)(2,1)S(1)} %get-tuple-element.15.refs_4_.refs_0_, bf16[528,128]{1,0:T(8,128)(2,1)S(1)} %collective-permute-done.3.refs_5_.refs_1_, ...), custom_call_target="tpu_custom_call" | custom-call | tf_op jit(solution)/shard_map/pallas_call | solution.py:343
  20.5 1.9 %collective-permute-start.6 = (bf16[512,128]{1,0:T(8,128)(2,1)S(1)}, bf16[512,128]{1,0:T(8,128)(2,1)S(1)}, u32[]{:S(2)}, u32[]{:S(2)}) collective-permute-start(bf16[512,128]{1,0:T(8,128)(2,1)S(1)} %get-tuple-element.20), channel_id=1, source_target_pairs={{0,4},{4,0},{8,12},{12,8},{16,20},{20,16},{24,28},{28,24},{1,5},{5... | collective-permute-start | bytes 393224 | tf_op jit(solution)/shard_map/ppermute | solution.py:283
  22.5 1.1 %collective-permute-start.7 = (bf16[512,128]{1,0:T(8,128)(2,1)S(1)}, bf16[512,128]{1,0:T(8,128)(2,1)S(1)}, u32[]{:S(2)}, u32[]{:S(2)}) collective-permute-start(bf16[512,128]{1,0:T(8,128)(2,1)S(1)} %get-tuple-element.21), channel_id=1, source_target_pairs={{0,8},{4,12},{8,0},{12,4},{16,24},{20,28},{24,16},{28,20},{1,9},{5... | collective-permute-start | bytes 393224 | tf_op jit(solution)/shard_map/ppermute | solution.py:283
  23.5 0.6 %collective-permute-start.8 = (bf16[512,128]{1,0:T(8,128)(2,1)S(1)}, bf16[512,128]{1,0:T(8,128)(2,1)S(1)}, u32[]{:S(2)}, u32[]{:S(2)}) collective-permute-start(bf16[512,128]{1,0:T(8,128)(2,1)S(1)} %get-tuple-element.22), channel_id=1, source_target_pairs={{0,12},{4,8},{8,4},{12,0},{16,28},{20,24},{24,20},{28,16},{1,13},{... | collective-permute-start | bytes 393224 | tf_op jit(solution)/shard_map/ppermute | solution.py:283
  24.1 0.6 %collective-permute-done.5.refs_8_ = bf16[512,128]{1,0:T(8,128)(2,1)S(1)} collective-permute-done((bf16[512,128]{1,0:T(8,128)(2,1)S(1)}, bf16[512,128]{1,0:T(8,128)(2,1)S(1)}, u32[]{:S(2)}, u32[]{:S(2)}) %collective-permute-start.5) | collective-permute-done | bytes 131104 | tf_op jit(solution)/shard_map/ppermute | solution.py:283
  24.7 0.9 %shard_map.88 = bf16[2,128,128]{2,1,0:T(8,128)(2,1)} custom-call(bf16[528,128]{1,0:T(8,128)(2,1)S(1)} %get-tuple-element.14.refs_0_, bf16[528,128]{1,0:T(8,128)(2,1)S(1)} %collective-permute-done.refs_1_, bf16[528,128]{1,0:T(8,128)(2,1)S(1)} %collective-permute-done.1.refs_2_, bf16[528,128]{1,0:T(8,128)(2,1)S(1)} %collective-permute-done.2.refs_3_, ...), custom_call_target="tpu_custom_call" | custom-call | tf_op jit(solution)/shard_map/pallas_call | solution.py:352
  25.6 0.6 %collective-permute-done.6.refs_1_ = bf16[512,128]{1,0:T(8,128)(2,1)S(1)} collective-permute-done((bf16[512,128]{1,0:T(8,128)(2,1)S(1)}, bf16[512,128]{1,0:T(8,128)(2,1)S(1)}, u32[]{:S(2)}, u32[]{:S(2)}) %collective-permute-start.6) | collective-permute-done | bytes 131104 | tf_op jit(solution)/shard_map/ppermute | solution.py:283
  26.2 1.2 %collective-permute-done.7.refs_2_ = bf16[512,128]{1,0:T(8,128)(2,1)S(1)} collective-permute-done((bf16[512,128]{1,0:T(8,128)(2,1)S(1)}, bf16[512,128]{1,0:T(8,128)(2,1)S(1)}, u32[]{:S(2)}, u32[]{:S(2)}) %collective-permute-start.7) | collective-permute-done | bytes 131104 | tf_op jit(solution)/shard_map/ppermute | solution.py:283
  27.4 2.0 %collective-permute-done.8.refs_3_ = bf16[512,128]{1,0:T(8,128)(2,1)S(1)} collective-permute-done((bf16[512,128]{1,0:T(8,128)(2,1)S(1)}, bf16[512,128]{1,0:T(8,128)(2,1)S(1)}, u32[]{:S(2)}, u32[]{:S(2)}) %collective-permute-start.8) | collective-permute-done | bytes 131104 | tf_op jit(solution)/shard_map/ppermute | solution.py:283
  29.4 0.7 %shard_map.90 = (bf16[2,128,128]{2,1,0:T(8,128)(2,1)}, bf16[2,128,128]{2,1,0:T(8,128)(2,1)}) custom-call(f32[512,128]{1,0:T(8,128)S(1)} %get-tuple-element.19.refs_0_, bf16[512,128]{1,0:T(8,128)(2,1)S(1)} %collective-permute-done.6.refs_1_, bf16[512,128]{1,0:T(8,128)(2,1)S(1)} %collective-permute-done.7.refs_2_, ...), custom_call_target="tpu_custom_call" | custom-call | tf_op jit(solution)/shard_map/pallas_call | solution.py:360
Async XLA Ops:
  1.6 7.2 %collective-permute-start.1 = (bf16[528,128]{1,0:T(8,128)(2,1)S(1)}, bf16[528,128]{1,0:T(8,128)(2,1)S(1)}, u32[]{:S(2)}, u32[]{:S(2)}) collective-permute-start(bf16[528,128]{1,0:T(8,128)(2,1)S(1)} %get-tuple-element.14.refs_0_), channel_id=1, source_target_pairs={{0,8},{4,12},{8,0},{12,4},{16,24},{20,28},{24,16},{28,20},{1,9},{5... | collective-permute-start | bytes 405512 | tf_op jit(solution)/shard_map/ppermute | solution.py:283
  4.7 10.1 %collective-permute-start = (bf16[528,128]{1,0:T(8,128)(2,1)S(1)}, bf16[528,128]{1,0:T(8,128)(2,1)S(1)}, u32[]{:S(2)}, u32[]{:S(2)}) collective-permute-start(bf16[528,128]{1,0:T(8,128)(2,1)S(1)} %get-tuple-element.14.refs_0_), channel_id=1, source_target_pairs={{0,4},{4,0},{8,12},{12,8},{16,20},{20,16},{24,28},{28,24},{1,5},{5... | collective-permute-start | bytes 405512 | tf_op jit(solution)/shard_map/ppermute | solution.py:283
  6.2 8.6 %collective-permute-start.3 = (bf16[528,128]{1,0:T(8,128)(2,1)S(1)}, bf16[528,128]{1,0:T(8,128)(2,1)S(1)}, u32[]{:S(2)}, u32[]{:S(2)}) collective-permute-start(bf16[528,128]{1,0:T(8,128)(2,1)S(1)} %get-tuple-element.15.refs_4_.refs_0_), channel_id=1, source_target_pairs={{0,16},{4,20},{8,24},{12,28},{16,0},{20,4},{24,8},{28,12},{1,17},{... | collective-permute-start | bytes 405512 | tf_op jit(solution)/shard_map/ppermute | solution.py:283
  8.8 6.0 %collective-permute-start.2 = (bf16[528,128]{1,0:T(8,128)(2,1)S(1)}, bf16[528,128]{1,0:T(8,128)(2,1)S(1)}, u32[]{:S(2)}, u32[]{:S(2)}) collective-permute-start(bf16[528,128]{1,0:T(8,128)(2,1)S(1)} %collective-permute-done.1.refs_2_), channel_id=1, source_target_pairs={{0,4},{4,0},{8,12},{12,8},{16,20},{20,16},{24,28},{28,24},{1,5},{5... | collective-permute-start | bytes 405512 | tf_op jit(solution)/shard_map/ppermute | solution.py:283
  15.4 4.6 %collective-permute-start.4 = (f32[8,256]{1,0:T(8,128)S(1)}, f32[8,256]{1,0:T(8,128)S(1)}, u32[]{:S(2)}, u32[]{:S(2)}) collective-permute-start(f32[8,256]{1,0:T(8,128)S(1)} %get-tuple-element.16.refs_4_.refs_2_), channel_id=1, source_target_pairs={{0,16},{4,20},{8,24},{12,28},{16,0},{20,4},{24,8},{28,12},{1,17},{... | collective-permute-start | bytes 24584 | tf_op jit(solution)/shard_map/ppermute | solution.py:283
  18.3 6.4 %collective-permute-start.5 = (bf16[512,128]{1,0:T(8,128)(2,1)S(1)}, bf16[512,128]{1,0:T(8,128)(2,1)S(1)}, u32[]{:S(2)}, u32[]{:S(2)}) collective-permute-start(bf16[512,128]{1,0:T(8,128)(2,1)S(1)} %shard_map.87), channel_id=1, source_target_pairs={{0,16},{4,20},{8,24},{12,28},{16,0},{20,4},{24,8},{28,12},{1,17},{... | collective-permute-start | bytes 393224 | tf_op jit(solution)/shard_map/ppermute | solution.py:283
  20.5 5.7 %collective-permute-start.6 = (bf16[512,128]{1,0:T(8,128)(2,1)S(1)}, bf16[512,128]{1,0:T(8,128)(2,1)S(1)}, u32[]{:S(2)}, u32[]{:S(2)}) collective-permute-start(bf16[512,128]{1,0:T(8,128)(2,1)S(1)} %get-tuple-element.20), channel_id=1, source_target_pairs={{0,4},{4,0},{8,12},{12,8},{16,20},{20,16},{24,28},{28,24},{1,5},{5... | collective-permute-start | bytes 393224 | tf_op jit(solution)/shard_map/ppermute | solution.py:283
  22.5 5.0 %collective-permute-start.7 = (bf16[512,128]{1,0:T(8,128)(2,1)S(1)}, bf16[512,128]{1,0:T(8,128)(2,1)S(1)}, u32[]{:S(2)}, u32[]{:S(2)}) collective-permute-start(bf16[512,128]{1,0:T(8,128)(2,1)S(1)} %get-tuple-element.21), channel_id=1, source_target_pairs={{0,8},{4,12},{8,0},{12,4},{16,24},{20,28},{24,16},{28,20},{1,9},{5... | collective-permute-start | bytes 393224 | tf_op jit(solution)/shard_map/ppermute | solution.py:283
  23.5 5.9 %collective-permute-start.8 = (bf16[512,128]{1,0:T(8,128)(2,1)S(1)}, bf16[512,128]{1,0:T(8,128)(2,1)S(1)}, u32[]{:S(2)}, u32[]{:S(2)}) collective-permute-start(bf16[512,128]{1,0:T(8,128)(2,1)S(1)} %get-tuple-element.22), channel_id=1, source_target_pairs={{0,12},{4,8},{8,4},{12,0},{16,28},{20,24},{24,20},{28,16},{1,13},{... | collective-permute-start | bytes 393224 | tf_op jit(solution)/shard_map/ppermute | solution.py:283
where the time goes:
time: 30.3 us; the launch traced here: 30.1 us
  starting transfers between devices  16.7 us (55%)
  waiting for transfers between devices  8.67 us (29%)
  Pallas kernels  4.08 us (13%)
  between operations  0.67 us (2%)
    ppermute x9, starting transfers between devices, exchanged(): lax.ppermute(value, 'seq', [(i, i ^ mask) for i in range(lax.axis_size('s...  16.7 us
    ppermute x9, waiting for transfers between devices, exchanged(): lax.ppermute(value, 'seq', [(i, i ^ mask) for i in range(lax.axis_size('s...  8.67 us
    pallas_call x1, Pallas kernels, gathered(): pl.pallas_call(functools.partial(pack_kernel, sizes), out_shape=(pltpu.VM...  0.96 us
    pallas_call x1, Pallas kernels, gathered(): pl.pallas_call(functools.partial(queries_kernel, sizes, widths), out_shap...  0.94 us
    pallas_call x1, Pallas kernels, gathered(): pl.pallas_call(functools.partial(sum_kernel, sizes, n_keys), out_shape=(o...  0.71 us
    pallas_call x1, Pallas kernels, gathered(): pl.pallas_call(functools.partial(stats_kernel, sizes, widths), out_shape=...  0.63 us
  transfers between devices with their start and end apart: 9, of which 6 were waited for; matrix products, arithmetic and copies ran while one was open for 0% of the time, Pallas kernels for 6%

commit v1 on v0

--- a/solution.py
+++ b/solution.py
@@ -125,7 +125,7 @@
             lax.dot_general(self.v(h, keys), self.g(h, queries), NT, preferred_element_type=jnp.float32),
         )
 
-    def stats(self, scored, bias, keep):
+    def stats(self, scored, bias, keep, start=None):
         s, dp = scored
         lanes = s.shape[1]
         steps = self.block_rows // 8
@@ -135,6 +135,8 @@
             x = jnp.max(x.reshape(steps, 8, lanes), axis=0)
             top = x if top is None else jnp.maximum(top, x)
         top = jnp.maximum(jnp.max(top, axis=0, keepdims=True), 0.5 * NEVER)
+        if start:
+            top = jnp.maximum(top, start[0])
         acc_l = acc_d = None
         for kb in range(bias.shape[0]):
             cut = slice(kb * self.block_rows, (kb + 1) * self.block_rows)
@@ -144,13 +146,17 @@
             e = jnp.sum(e.reshape(steps, 8, lanes), axis=0)
             acc_l = e if acc_l is None else acc_l + e
             acc_d = d if acc_d is None else acc_d + d
-        return top, jnp.sum(acc_l, axis=0, keepdims=True), jnp.sum(acc_d, axis=0, keepdims=True)
-
-
-def stats_kernel(sizes, widths, *refs):
-    n_keys, n_queries = widths
+        acc_l, acc_d = (jnp.sum(x, axis=0, keepdims=True) for x in (acc_l, acc_d))
+        if start:
+            w = jnp.exp2(start[0] - top)
+            acc_l, acc_d = acc_l + start[1] * w, acc_d + start[2] * w
+        return top, acc_l, acc_d
+
+
+def stats_kernel(sizes, n_keys, n_queries, *refs):
     a_refs, b_refs = refs[:n_keys], refs[n_keys : n_keys + n_queries]
-    stat, e_ref, dp_ref = refs[n_keys + n_queries :]
+    before = refs[n_keys + n_queries : -3]
+    stat, e_ref, dp_ref = refs[-3:]
     sh = Shards(sizes, a_refs, b_refs)
     keys, queries = list(range(n_keys)), list(range(n_queries))
     bias = sh.bias(sh.key_ids(keys), queries)
@@ -161,15 +167,29 @@
             e_ref[h, cut] = e
             dp_ref[h, cut] = dp
 
-        for i, x in enumerate(sh.stats(scored[h], bias[h], keep)):
+        start = [before[0][3 * h + i : 3 * h + i + 1] for i in range(3)] if before else None
+        for i, x in enumerate(sh.stats(scored[h], bias[h], keep, start)):
             stat[3 * h + i : 3 * h + i + 1] = x
+
+
+def kept_tiles(sh, kept, stat, h, lanes, shift=None):
+    first, e_first, dp_first, e_last, dp_last = kept
+    row = slice(3 * h, 3 * h + 1)
+    top = stat[row, lanes]
+    base = top if shift is None else shift
+    for before, e_ref, dp_ref in ((first[row, lanes], e_first, dp_first), (top, e_last, dp_last)):
+        w = None if before is base else jnp.exp2(before - base)
+        for r in range(0, e_ref.shape[1], sh.block_rows):
+            cut = slice(r, r + sh.block_rows)
+            e = e_ref[h, cut, lanes]
+            yield (e if w is None else e * w), dp_ref[h, cut, lanes]
 
 
 def partner_kernel(sizes, widths, *refs):
     heads, rows = sizes[0], sizes[2]
     n_keys, n_queries = widths
-    a_refs, (stat, e_ref, dp_ref) = refs[:n_keys], refs[n_keys : n_keys + 3]
-    outs = refs[n_keys + 3 :]
+    a_refs, stat, kept = refs[:n_keys], refs[n_keys], refs[n_keys + 1 : n_keys + 6]
+    outs = refs[n_keys + 6 :]
     sh = Shards(sizes, a_refs, ())
     tn = (((0,), (0,)), ((), ()))
     for s in range(1, n_queries):
@@ -178,10 +198,9 @@
             k = sh.k(h, list(range(n_keys)))
             local = local_dot(stat, h, lanes)
             low, e_low = [], []
-            for r in range(0, n_keys * rows, sh.block_rows):
-                e = e_ref[h, r : r + sh.block_rows, lanes]
+            for e, dp in kept_tiles(sh, kept, stat, h, lanes):
                 e_low.append(e.astype(jnp.bfloat16))
-                low.append((e * (dp_ref[h, r : r + sh.block_rows, lanes] - local)).astype(jnp.bfloat16))
+                low.append((e * (dp - local)).astype(jnp.bfloat16))
             for i, x in enumerate((low, e_low)):
                 x = lax.dot_general(jnp.concatenate(x), k, tn, preferred_element_type=jnp.float32)
                 outs[s - 1][(i * heads + h) * rows : (i * heads + h + 1) * rows] = x.astype(outs[s - 1].dtype)
@@ -209,20 +228,17 @@
     heads, rows = sizes[0], sizes[2]
     n_keys, n_queries = widths
     b_refs = refs[:n_queries]
-    stats, (e_ref, dp_ref) = refs[n_queries : 2 * n_queries], refs[2 * n_queries : 2 * n_queries + 2]
-    kv_out = refs[2 * n_queries + 2 :]
+    stats, kept = refs[n_queries : 2 * n_queries], refs[2 * n_queries : 2 * n_queries + 5]
+    kv_out = refs[2 * n_queries + 5 :]
     sh = Shards(sizes, (), b_refs)
     queries = list(range(n_queries))
     for h in range(heads):
         whole = [whole_stats(stats, rows, h, s) for s in queries]
         shift, dots = (jnp.concatenate([x[i] for x in whole], axis=1) for i in range(2))
-        w = jnp.exp2(stats[0][3 * h : 3 * h + 1] - shift)
         p_low, ds_low = [], []
-        for r in range(0, n_keys * rows, sh.block_rows):
-            cut = slice(r, r + sh.block_rows)
-            p = e_ref[h, cut] * w
+        for p, dp in kept_tiles(sh, kept, stats[0], h, slice(0, n_queries * rows), shift):
             p_low.append(p.astype(jnp.bfloat16))
-            ds_low.append((p * (dp_ref[h, cut] - dots)).astype(jnp.bfloat16))
+            ds_low.append((p * (dp - dots)).astype(jnp.bfloat16))
         dk = jnp.dot(jnp.concatenate(ds_low), sh.q(h, queries), preferred_element_type=jnp.float32) * sh.scale
         dv = jnp.dot(jnp.concatenate(p_low), sh.g(h, queries), preferred_element_type=jnp.float32)
         for m in range(n_keys):
@@ -235,16 +251,14 @@
     heads, rows = sizes[0], sizes[2]
     n_keys, n_queries = widths
     a_refs, refs = refs[:n_keys], refs[n_keys:]
-    stats, (e_ref, dp_ref), refs = refs[:n_queries], refs[n_queries : n_queries + 2], refs[n_queries + 2 :]
+    stats, kept, refs = refs[:n_queries], refs[n_queries : n_queries + 5], refs[n_queries + 5 :]
     sums, out = refs[: n_queries - 1], refs[-1]
     sh = Shards(sizes, a_refs, ())
     for h in range(heads):
         shift, dots = whole_stats(stats, rows, h, 0)
-        w = jnp.exp2(stats[0][3 * h : 3 * h + 1, 0:rows] - shift)
         low = []
-        for r in range(0, n_keys * rows, sh.block_rows):
-            cut = slice(r, r + sh.block_rows)
-            low.append(((e_ref[h, cut, 0:rows] * w) * (dp_ref[h, cut, 0:rows] - dots)).astype(jnp.bfloat16))
+        for p, dp in kept_tiles(sh, kept, stats[0], h, slice(0, rows), shift):
+            low.append((p * (dp - dots)).astype(jnp.bfloat16))
         dq = lax.dot_general(
             jnp.concatenate(low), sh.k(h, list(range(n_keys))), (((0,), (0,)), ((), ())),
             preferred_element_type=jnp.float32,
@@ -321,22 +335,30 @@
     a_all = [a_all[m] for m in range(n_keys)]
     lanes = n_queries * rows
     stat_rows = -(-3 * heads // 8) * 8
-    stat, e, dp = pl.pallas_call(
-        functools.partial(stats_kernel, sizes, widths),
-        out_shape=(pltpu.VMEM((stat_rows, lanes), jnp.float32),)
-        + (pltpu.VMEM((heads, n_keys * rows, lanes), jnp.float32),) * 2,
-        compiler_params=params,
-        in_specs=[vmem] * count_of(widths),
-        out_specs=(vmem,) * 3,
-    )(*near(a_all), *near(b_all))
+    a_all = near([a_all[0]] + [a_all[m] for moves in key_moves(n_keys) for m in sorted(m for m, _ in moves)])
+    b_all = near(b_all)
+    n_first = 1 + len(key_moves(n_keys)[0])
+    stat, kept = None, []
+    for part in (a_all[:n_first], a_all[n_first:]):
+        before = near([stat]) if kept else []
+        stat, e, dp = pl.pallas_call(
+            functools.partial(stats_kernel, sizes, len(part), n_queries),
+            out_shape=(pltpu.VMEM((stat_rows, lanes), jnp.float32),)
+            + (pltpu.VMEM((heads, len(part) * rows, lanes), jnp.float32),) * 2,
+            compiler_params=params,
+            in_specs=[vmem] * (len(part) + n_queries + len(before)),
+            out_specs=(vmem,) * 3,
+        )(*part, *b_all, *before)
+        kept += ([] if kept else [stat]) + [e, dp]
+    kept = near(kept)
     stats = [stat] + [exchanged(stat, s * n_keys) for s in range(1, n_queries)]
     sums = pl.pallas_call(
         functools.partial(partner_kernel, sizes, widths),
         out_shape=(pltpu.VMEM((2 * heads * rows, width), queries.dtype),) * (n_queries - 1),
         compiler_params=params,
-        in_specs=[vmem] * (n_keys + 3),
+        in_specs=[vmem] * (n_keys + 6),
         out_specs=(vmem,) * (n_queries - 1),
-    )(*near(a_all), *near([stat, e, dp]))
+    )(*a_all, *near([stat]), *kept)
     sums = [exchanged(x, s * n_keys) for s, x in zip(range(1, n_queries), sums)]
     shapes = [pltpu.VMEM((2 * heads * rows, width), jnp.float32)]
     shapes += [pltpu.VMEM((2 * heads * rows, width), queries.dtype)] * (n_keys - 1)
@@ -344,18 +366,19 @@
         functools.partial(grads_kernel, sizes, widths),
         out_shape=tuple(shapes),
         compiler_params=params,
-        in_specs=[vmem] * (2 * n_queries + 2),
+        in_specs=[vmem] * (2 * n_queries + 5),
         out_specs=(vmem,) * len(shapes),
-    )(*near(b_all), *near(stats), *near([e, dp]))
-    parts = [parts[0]] + [exchanged(parts[m], m) for m in range(1, n_keys)]
+    )(*b_all, *near(stats), *kept)
+    order = [m for moves in key_moves(n_keys) for m in sorted(m for m, _ in moves)]
+    parts = [parts[0]] + [exchanged(x, m) for m, x in zip(order, parts[1:])]
     out = jax.ShapeDtypeStruct(queries.shape, queries.dtype)
     grad_queries = pl.pallas_call(
         functools.partial(queries_kernel, sizes, widths),
         out_shape=out,
         compiler_params=params,
-        in_specs=[vmem] * (n_keys + 2 * n_queries + 1),
+        in_specs=[vmem] * (n_keys + 2 * n_queries + 4),
         out_specs=vmem,
-    )(*near(a_all), *near(stats), *near([e, dp]), *near(sums))
+    )(*a_all, *near(stats), *kept, *near(sums))
     buf = pltpu.VMEM(queries.shape, queries.dtype)
     grad_keys, grad_values = pl.pallas_call(
         functools.partial(sum_kernel, sizes, n_keys),
@@ -366,10 +389,6 @@
         scratch_shapes=[buf, buf, pltpu.SemaphoreType.DMA((2,))],
     )(*near(parts))
     return grad_queries, grad_keys, grad_values
-
-
-def count_of(widths):
-    return widths[0] + widths[1]
 
 
 def with_halo(value, sides, width):
@@ -544,7 +563,7 @@
     count = lax.axis_size("seq")
     rows, width = queries.shape[1:]
     gathered_bytes = 4 * count * queries.size * queries.dtype.itemsize
-    if gathered_bytes <= GATHER_BYTES and count & (count - 1) == 0 and rows == width:
+    if gathered_bytes <= GATHER_BYTES and count & (count - 1) == 0 and count > GROUP and rows == width:
         return gathered(queries, keys, values, grad_out, rand_ids, global_ids)
     return routed(queries, keys, values, grad_out, rand_ids, global_ids)
 

time: 30.3 us -> 30.2 us (level)
  starting transfers between devices: 16.7 us -> 15.7 us
  waiting for transfers between devices: 8.67 us -> 9.43 us
    ppermute x9, starting transfers between devices: 16.7 us -> 15.7 us  [exchanged(): lax.ppermute(value, 'seq', [(i, i ^ mask) for i in range(lax.axis_size('s...]
    ppermute x9, waiting for transfers between devices: 8.67 us -> 9.43 us  [exchanged(): lax.ppermute(value, 'seq', [(i, i ^ mask) for i in range(lax.axis_size('s...]
    pallas_call x1 -> x2, Pallas kernels: 0.63 us -> 0.81 us  [gathered(): pl.pallas_call(functools.partial(stats_kernel, sizes, len(part), n_querie...]
  transfers between devices with their start and end apart: 9 -> 9, of which waited for: 6 -> 7; matrix products, arithmetic and copies ran while one was open for 0% -> 0% of each run, Pallas kernels for 6% -> 8%
where the time goes in v1:
time: 30.2 us; the launch traced here: 30 us
  starting transfers between devices  15.7 us (52%)
  waiting for transfers between devices  9.43 us (31%)
  Pallas kernels  4.25 us (14%)
  between operations  0.67 us (2%)
    ppermute x9, starting transfers between devices, exchanged(): lax.ppermute(value, 'seq', [(i, i ^ mask) for i in range(lax.axis_size('s...  15.7 us
    ppermute x9, waiting for transfers between devices, exchanged(): lax.ppermute(value, 'seq', [(i, i ^ mask) for i in range(lax.axis_size('s...  9.43 us
    pallas_call x1, Pallas kernels, gathered(): pl.pallas_call(functools.partial(pack_kernel, sizes), out_shape=(pltpu.VM...  0.96 us
    pallas_call x1, Pallas kernels, gathered(): pl.pallas_call(functools.partial(queries_kernel, sizes, widths), out_shap...  0.94 us
    pallas_call x2, Pallas kernels, gathered(): pl.pallas_call(functools.partial(stats_kernel, sizes, len(part), n_querie...  0.81 us
    pallas_call x1, Pallas kernels, gathered(): pl.pallas_call(functools.partial(sum_kernel, sizes, n_keys), out_shape=(o...  0.71 us
  transfers between devices with their start and end apart: 9, of which 7 were waited for; matrix products, arithmetic and copies ran while one was open for 0% of the time, Pallas kernels for 8%

profile of v1, /device:TPU:0, one launch (start us, length us, event | category | flops | bytes accessed | tf_op | source)
XLA Modules:
  0.0 30.0 jit_solution(17012099905242267040)
XLA Ops:
  0.6 1.0 %shard_map.85 = (bf16[528,128]{1,0:T(8,128)(2,1)S(1)}, bf16[528,128]{1,0:T(8,128)(2,1)S(1)}) custom-call(s32[2,2,3]{2,1,0:T(2,128)} %ids_hbm.1, s32[2]{0:T(128)} %gids_hbm.1, bf16[2,128,128]{2,1,0:T(8,128)(2,1)} %k_ref.1, bf16[2,128,128]{2,1,0:T(8,128)(2,1)} %v_ref.1, bf16[2,128,128]{2,1,0:T(8,128)(2,1)} %q_ref.1, bf16[2,128,128]{2,1,0:T(8,128)(2,1)} %g_ref.1), custom_call_target="tpu_custom_call" | custom-call | tf_op jit(solution)/shard_map/pallas_call | solution.py:318
  1.6 3.1 %collective-permute-start.1 = (bf16[528,128]{1,0:T(8,128)(2,1)S(1)}, bf16[528,128]{1,0:T(8,128)(2,1)S(1)}, u32[]{:S(2)}, u32[]{:S(2)}) collective-permute-start(bf16[528,128]{1,0:T(8,128)(2,1)S(1)} %get-tuple-element.17.refs_0_), channel_id=1, source_target_pairs={{0,8},{4,12},{8,0},{12,4},{16,24},{20,28},{24,16},{28,20},{1,9},{5... | collective-permute-start | bytes 405512 | tf_op jit(solution)/shard_map/ppermute | solution.py:297
  4.7 2.6 %collective-permute-start.3 = (bf16[528,128]{1,0:T(8,128)(2,1)S(1)}, bf16[528,128]{1,0:T(8,128)(2,1)S(1)}, u32[]{:S(2)}, u32[]{:S(2)}) collective-permute-start(bf16[528,128]{1,0:T(8,128)(2,1)S(1)} %get-tuple-element.18.refs_3_.refs_1_.refs_0_), channel_id=1, source_target_pairs={{0,16},{4,20},{8,24},{12,28},{16,0},{20,4},{24,8},{28,12},{1,17},{... | collective-permute-start | bytes 405512 | tf_op jit(solution)/shard_map/ppermute | solution.py:297
  7.3 1.5 %collective-permute-start = (bf16[528,128]{1,0:T(8,128)(2,1)S(1)}, bf16[528,128]{1,0:T(8,128)(2,1)S(1)}, u32[]{:S(2)}, u32[]{:S(2)}) collective-permute-start(bf16[528,128]{1,0:T(8,128)(2,1)S(1)} %get-tuple-element.17.refs_0_), channel_id=1, source_target_pairs={{0,4},{4,0},{8,12},{12,8},{16,20},{20,16},{24,28},{28,24},{1,5},{5... | collective-permute-start | bytes 405512 | tf_op jit(solution)/shard_map/ppermute | solution.py:297
  8.8 1.5 %collective-permute-done.1.refs_2_ = bf16[528,128]{1,0:T(8,128)(2,1)S(1)} collective-permute-done((bf16[528,128]{1,0:T(8,128)(2,1)S(1)}, bf16[528,128]{1,0:T(8,128)(2,1)S(1)}, u32[]{:S(2)}, u32[]{:S(2)}) %collective-permute-start.1) | collective-permute-done | bytes 135200 | tf_op jit(solution)/shard_map/ppermute | solution.py:297
  10.3 1.8 %collective-permute-start.2 = (bf16[528,128]{1,0:T(8,128)(2,1)S(1)}, bf16[528,128]{1,0:T(8,128)(2,1)S(1)}, u32[]{:S(2)}, u32[]{:S(2)}) collective-permute-start(bf16[528,128]{1,0:T(8,128)(2,1)S(1)} %collective-permute-done.1.refs_2_), channel_id=1, source_target_pairs={{0,4},{4,0},{8,12},{12,8},{16,20},{20,16},{24,28},{28,24},{1,5},{5... | collective-permute-start | bytes 405512 | tf_op jit(solution)/shard_map/ppermute | solution.py:297
  12.2 1.4 %collective-permute-done.3.refs_4_.refs_2_.refs_1_ = bf16[528,128]{1,0:T(8,128)(2,1)S(1)} collective-permute-done((bf16[528,128]{1,0:T(8,128)(2,1)S(1)}, bf16[528,128]{1,0:T(8,128)(2,1)S(1)}, u32[]{:S(2)}, u32[]{:S(2)}) %collective-permute-start.3) | collective-permute-done | bytes 135200 | tf_op jit(solution)/shard_map/ppermute | solution.py:297
  13.6 0.0 collective-permute-done.refs_1_
  13.6 0.5 %shard_map.86 = (f32[8,256]{1,0:T(8,128)S(1)}, f32[2,384,256]{2,1,0:T(8,128)S(1)}, f32[2,384,256]{2,1,0:T(8,128)S(1)}) custom-call(bf16[528,128]{1,0:T(8,128)(2,1)S(1)} %get-tuple-element.17.refs_0_, bf16[528,128]{1,0:T(8,128)(2,1)S(1)} %collective-permute-done.refs_1_, bf16[528,128]{1,0:T(8,128)(2,1)S(1)} %collective-permute-done.1.refs_2_, ...), custom_call_target="tpu_custom_call" | custom-call | tf_op jit(solution)/shard_map/pallas_call | solution.py:344
  14.1 1.2 %collective-permute-done.2.refs_0_.refs_3_ = bf16[528,128]{1,0:T(8,128)(2,1)S(1)} collective-permute-done((bf16[528,128]{1,0:T(8,128)(2,1)S(1)}, bf16[528,128]{1,0:T(8,128)(2,1)S(1)}, u32[]{:S(2)}, u32[]{:S(2)}) %collective-permute-start.2) | collective-permute-done | bytes 135200 | tf_op jit(solution)/shard_map/ppermute | solution.py:297
  15.4 0.3 %shard_map.87 = (f32[8,256]{1,0:T(8,128)S(1)}, f32[2,128,256]{2,1,0:T(8,128)S(1)}, f32[2,128,256]{2,1,0:T(8,128)S(1)}) custom-call(bf16[528,128]{1,0:T(8,128)(2,1)S(1)} %collective-permute-done.2.refs_0_.refs_3_, bf16[528,128]{1,0:T(8,128)(2,1)S(1)} %get-tuple-element.18.refs_3_.refs_1_.refs_0_, ...), custom_call_target="tpu_custom_call" | custom-call | tf_op jit(solution)/shard_map/pallas_call | solution.py:344
  15.7 1.9 %collective-permute-start.4 = (f32[8,256]{1,0:T(8,128)S(1)}, f32[8,256]{1,0:T(8,128)S(1)}, u32[]{:S(2)}, u32[]{:S(2)}) collective-permute-start(f32[8,256]{1,0:T(8,128)S(1)} %get-tuple-element.20.refs_4_.refs_2_), channel_id=1, source_target_pairs={{0,16},{4,20},{8,24},{12,28},{16,0},{20,4},{24,8},{28,12},{1,17},{... | collective-permute-start | bytes 24584 | tf_op jit(solution)/shard_map/ppermute | solution.py:297
  17.6 0.4 %shard_map.88 = bf16[512,128]{1,0:T(8,128)(2,1)S(1)} custom-call(bf16[528,128]{1,0:T(8,128)(2,1)S(1)} %get-tuple-element.17.refs_0_, bf16[528,128]{1,0:T(8,128)(2,1)S(1)} %collective-permute-done.refs_1_, bf16[528,128]{1,0:T(8,128)(2,1)S(1)} %collective-permute-done.1.refs_2_, bf16[528,128]{1,0:T(8,128)(2,1)S(1)} %collective-permute-done.2.refs_0_.refs_3_, ...), custom_call_target="tpu_custom_call" | custom-call | tf_op jit(solution)/shard_map/pallas_call | solution.py:355
  17.9 1.1 %collective-permute-start.5 = (bf16[512,128]{1,0:T(8,128)(2,1)S(1)}, bf16[512,128]{1,0:T(8,128)(2,1)S(1)}, u32[]{:S(2)}, u32[]{:S(2)}) collective-permute-start(bf16[512,128]{1,0:T(8,128)(2,1)S(1)} %shard_map.88), channel_id=1, source_target_pairs={{0,16},{4,20},{8,24},{12,28},{16,0},{20,4},{24,8},{28,12},{1,17},{... | collective-permute-start | bytes 393224 | tf_op jit(solution)/shard_map/ppermute | solution.py:297
  19.1 1.2 %collective-permute-done.4.refs_5_.refs_3_ = f32[8,256]{1,0:T(8,128)S(1)} collective-permute-done((f32[8,256]{1,0:T(8,128)S(1)}, f32[8,256]{1,0:T(8,128)S(1)}, u32[]{:S(2)}, u32[]{:S(2)}) %collective-permute-start.4) | collective-permute-done | bytes 8224 | tf_op jit(solution)/shard_map/ppermute | solution.py:297
  20.3 0.5 %shard_map.90 = (f32[512,128]{1,0:T(8,128)S(1)}, bf16[512,128]{1,0:T(8,128)(2,1)S(1)}, bf16[512,128]{1,0:T(8,128)(2,1)S(1)}, bf16[512,128]{1,0:T(8,128)(2,1)S(1)}) custom-call(bf16[528,128]{1,0:T(8,128)(2,1)S(1)} %get-tuple-element.18.refs_3_.refs_1_.refs_0_, bf16[528,128]{1,0:T(8,128)(2,1)S(1)} %collective-permute-done.3.refs_4_.refs_2_.refs_1_, ...), custom_call_target="tpu_custom_call" | custom-call | tf_op jit(solution)/shard_map/pallas_call | solution.py:365
  20.7 2.0 %collective-permute-start.6 = (bf16[512,128]{1,0:T(8,128)(2,1)S(1)}, bf16[512,128]{1,0:T(8,128)(2,1)S(1)}, u32[]{:S(2)}, u32[]{:S(2)}) collective-permute-start(bf16[512,128]{1,0:T(8,128)(2,1)S(1)} %get-tuple-element.26), channel_id=1, source_target_pairs={{0,4},{4,0},{8,12},{12,8},{16,20},{20,16},{24,28},{28,24},{1,5},{5... | collective-permute-start | bytes 393224 | tf_op jit(solution)/shard_map/ppermute | solution.py:297
  22.8 0.7 %collective-permute-start.7 = (bf16[512,128]{1,0:T(8,128)(2,1)S(1)}, bf16[512,128]{1,0:T(8,128)(2,1)S(1)}, u32[]{:S(2)}, u32[]{:S(2)}) collective-permute-start(bf16[512,128]{1,0:T(8,128)(2,1)S(1)} %get-tuple-element.27), channel_id=1, source_target_pairs={{0,8},{4,12},{8,0},{12,4},{16,24},{20,28},{24,16},{28,20},{1,9},{5... | collective-permute-start | bytes 393224 | tf_op jit(solution)/shard_map/ppermute | solution.py:297
  23.4 0.8 %collective-permute-start.8 = (bf16[512,128]{1,0:T(8,128)(2,1)S(1)}, bf16[512,128]{1,0:T(8,128)(2,1)S(1)}, u32[]{:S(2)}, u32[]{:S(2)}) collective-permute-start(bf16[512,128]{1,0:T(8,128)(2,1)S(1)} %get-tuple-element.28), channel_id=1, source_target_pairs={{0,12},{4,8},{8,4},{12,0},{16,28},{20,24},{24,20},{28,16},{1,13},{... | collective-permute-start | bytes 393224 | tf_op jit(solution)/shard_map/ppermute | solution.py:297
  24.3 0.0 collective-permute-done.5.refs_11_
  24.3 0.9 %shard_map.89 = bf16[2,128,128]{2,1,0:T(8,128)(2,1)} custom-call(bf16[528,128]{1,0:T(8,128)(2,1)S(1)} %get-tuple-element.17.refs_0_, bf16[528,128]{1,0:T(8,128)(2,1)S(1)} %collective-permute-done.refs_1_, bf16[528,128]{1,0:T(8,128)(2,1)S(1)} %collective-permute-done.1.refs_2_, bf16[528,128]{1,0:T(8,128)(2,1)S(1)} %collective-permute-done.2.refs_0_.refs_3_, ...), custom_call_target="tpu_custom_call" | custom-call | tf_op jit(solution)/shard_map/pallas_call | solution.py:375
  25.2 1.7 %collective-permute-done.6.refs_1_ = bf16[512,128]{1,0:T(8,128)(2,1)S(1)} collective-permute-done((bf16[512,128]{1,0:T(8,128)(2,1)S(1)}, bf16[512,128]{1,0:T(8,128)(2,1)S(1)}, u32[]{:S(2)}, u32[]{:S(2)}) %collective-permute-start.6) | collective-permute-done | bytes 131104 | tf_op jit(solution)/shard_map/ppermute | solution.py:297
  26.9 0.8 %collective-permute-done.7.refs_2_ = bf16[512,128]{1,0:T(8,128)(2,1)S(1)} collective-permute-done((bf16[512,128]{1,0:T(8,128)(2,1)S(1)}, bf16[512,128]{1,0:T(8,128)(2,1)S(1)}, u32[]{:S(2)}, u32[]{:S(2)}) %collective-permute-start.7) | collective-permute-done | bytes 131104 | tf_op jit(solution)/shard_map/ppermute | solution.py:297
  27.7 1.6 %collective-permute-done.8.refs_3_ = bf16[512,128]{1,0:T(8,128)(2,1)S(1)} collective-permute-done((bf16[512,128]{1,0:T(8,128)(2,1)S(1)}, bf16[512,128]{1,0:T(8,128)(2,1)S(1)}, u32[]{:S(2)}, u32[]{:S(2)}) %collective-permute-start.8) | collective-permute-done | bytes 131104 | tf_op jit(solution)/shard_map/ppermute | solution.py:297
  29.3 0.7 %shard_map.91 = (bf16[2,128,128]{2,1,0:T(8,128)(2,1)}, bf16[2,128,128]{2,1,0:T(8,128)(2,1)}) custom-call(f32[512,128]{1,0:T(8,128)S(1)} %get-tuple-element.25.refs_0_, bf16[512,128]{1,0:T(8,128)(2,1)S(1)} %collective-permute-done.6.refs_1_, bf16[512,128]{1,0:T(8,128)(2,1)S(1)} %collective-permute-done.7.refs_2_, ...), custom_call_target="tpu_custom_call" | custom-call | tf_op jit(solution)/shard_map/pallas_call | solution.py:383
Async XLA Ops:
  1.6 8.7 %collective-permute-start.1 = (bf16[528,128]{1,0:T(8,128)(2,1)S(1)}, bf16[528,128]{1,0:T(8,128)(2,1)S(1)}, u32[]{:S(2)}, u32[]{:S(2)}) collective-permute-start(bf16[528,128]{1,0:T(8,128)(2,1)S(1)} %get-tuple-element.17.refs_0_), channel_id=1, source_target_pairs={{0,8},{4,12},{8,0},{12,4},{16,24},{20,28},{24,16},{28,20},{1,9},{5... | collective-permute-start | bytes 405512 | tf_op jit(solution)/shard_map/ppermute | solution.py:297
  4.7 8.9 %collective-permute-start.3 = (bf16[528,128]{1,0:T(8,128)(2,1)S(1)}, bf16[528,128]{1,0:T(8,128)(2,1)S(1)}, u32[]{:S(2)}, u32[]{:S(2)}) collective-permute-start(bf16[528,128]{1,0:T(8,128)(2,1)S(1)} %get-tuple-element.18.refs_3_.refs_1_.refs_0_), channel_id=1, source_target_pairs={{0,16},{4,20},{8,24},{12,28},{16,0},{20,4},{24,8},{28,12},{1,17},{... | collective-permute-start | bytes 405512 | tf_op jit(solution)/shard_map/ppermute | solution.py:297
  7.3 6.3 %collective-permute-start = (bf16[528,128]{1,0:T(8,128)(2,1)S(1)}, bf16[528,128]{1,0:T(8,128)(2,1)S(1)}, u32[]{:S(2)}, u32[]{:S(2)}) collective-permute-start(bf16[528,128]{1,0:T(8,128)(2,1)S(1)} %get-tuple-element.17.refs_0_), channel_id=1, source_target_pairs={{0,4},{4,0},{8,12},{12,8},{16,20},{20,16},{24,28},{28,24},{1,5},{5... | collective-permute-start | bytes 405512 | tf_op jit(solution)/shard_map/ppermute | solution.py:297
  10.3 5.0 %collective-permute-start.2 = (bf16[528,128]{1,0:T(8,128)(2,1)S(1)}, bf16[528,128]{1,0:T(8,128)(2,1)S(1)}, u32[]{:S(2)}, u32[]{:S(2)}) collective-permute-start(bf16[528,128]{1,0:T(8,128)(2,1)S(1)} %collective-permute-done.1.refs_2_), channel_id=1, source_target_pairs={{0,4},{4,0},{8,12},{12,8},{16,20},{20,16},{24,28},{28,24},{1,5},{5... | collective-permute-start | bytes 405512 | tf_op jit(solution)/shard_map/ppermute | solution.py:297
  15.7 4.6 %collective-permute-start.4 = (f32[8,256]{1,0:T(8,128)S(1)}, f32[8,256]{1,0:T(8,128)S(1)}, u32[]{:S(2)}, u32[]{:S(2)}) collective-permute-start(f32[8,256]{1,0:T(8,128)S(1)} %get-tuple-element.20.refs_4_.refs_2_), channel_id=1, source_target_pairs={{0,16},{4,20},{8,24},{12,28},{16,0},{20,4},{24,8},{28,12},{1,17},{... | collective-permute-start | bytes 24584 | tf_op jit(solution)/shard_map/ppermute | solution.py:297
  17.9 6.4 %collective-permute-start.5 = (bf16[512,128]{1,0:T(8,128)(2,1)S(1)}, bf16[512,128]{1,0:T(8,128)(2,1)S(1)}, u32[]{:S(2)}, u32[]{:S(2)}) collective-permute-start(bf16[512,128]{1,0:T(8,128)(2,1)S(1)} %shard_map.88), channel_id=1, source_target_pairs={{0,16},{4,20},{8,24},{12,28},{16,0},{20,4},{24,8},{28,12},{1,17},{... | collective-permute-start | bytes 393224 | tf_op jit(solution)/shard_map/ppermute | solution.py:297
  20.7 6.2 %collective-permute-start.6 = (bf16[512,128]{1,0:T(8,128)(2,1)S(1)}, bf16[512,128]{1,0:T(8,128)(2,1)S(1)}, u32[]{:S(2)}, u32[]{:S(2)}) collective-permute-start(bf16[512,128]{1,0:T(8,128)(2,1)S(1)} %get-tuple-element.26), channel_id=1, source_target_pairs={{0,4},{4,0},{8,12},{12,8},{16,20},{20,16},{24,28},{28,24},{1,5},{5... | collective-permute-start | bytes 393224 | tf_op jit(solution)/shard_map/ppermute | solution.py:297
  22.8 5.0 %collective-permute-start.7 = (bf16[512,128]{1,0:T(8,128)(2,1)S(1)}, bf16[512,128]{1,0:T(8,128)(2,1)S(1)}, u32[]{:S(2)}, u32[]{:S(2)}) collective-permute-start(bf16[512,128]{1,0:T(8,128)(2,1)S(1)} %get-tuple-element.27), channel_id=1, source_target_pairs={{0,8},{4,12},{8,0},{12,4},{16,24},{20,28},{24,16},{28,20},{1,9},{5... | collective-permute-start | bytes 393224 | tf_op jit(solution)/shard_map/ppermute | solution.py:297
  23.4 5.9 %collective-permute-start.8 = (bf16[512,128]{1,0:T(8,128)(2,1)S(1)}, bf16[512,128]{1,0:T(8,128)(2,1)S(1)}, u32[]{:S(2)}, u32[]{:S(2)}) collective-permute-start(bf16[512,128]{1,0:T(8,128)(2,1)S(1)} %get-tuple-element.28), channel_id=1, source_target_pairs={{0,12},{4,8},{8,4},{12,0},{16,28},{20,24},{24,20},{28,16},{1,13},{... | collective-permute-start | bytes 393224 | tf_op jit(solution)/shard_map/ppermute | solution.py:297

commit v2 on v1

--- a/solution.py
+++ b/solution.py
@@ -29,21 +29,17 @@
         ((k_ref, a_ref, 0), (v_ref, a_ref, heads), (q_ref, b_ref, 0), (g_ref, b_ref, heads))
     ):
         for h in range(heads):
-            copies.append(
-                pltpu.make_async_copy(
-                    src.at[h], dst.at[pl.ds((first + h) * rows, rows)], sems.at[2 + i * heads + h]
-                )
-            )
+            place = pl.ds((first + h) * rows, rows)
+            copies.append(pltpu.make_async_copy(src.at[h], dst.at[place], sems.at[2 + i * heads + h]))
     for c in small + copies:
         c.start()
-    head_rows = a_ref.shape[0] - 2 * heads * rows
-    row = lax.broadcasted_iota(jnp.int32, (head_rows, rows), 0)
-    lane = lax.broadcasted_iota(jnp.int32, (head_rows, rows), 1)
-    me = lax.axis_index("seq")
+    shape = (b_ref.shape[0] - 2 * heads * rows, rows)
+    row = lax.broadcasted_iota(jnp.int32, shape, 0)
+    lane = lax.broadcasted_iota(jnp.int32, shape, 1)
     block = jnp.zeros_like(lane)
     for n in range(1, blocks):
         block = block + jnp.where(lane >= n * block_rows, 1, 0)
-    tile = me * blocks + block
+    tile = lax.axis_index("seq") * blocks + block
     for c in small:
         c.wait()
     for h in range(heads):
@@ -54,7 +50,6 @@
             tile = jnp.where(row == h * slots + j, ids, tile)
     for n in range(gids_ref.shape[0]):
         tile = jnp.where(row == heads * slots + 1 + n, gids_ref[n], tile)
-    a_ref[2 * heads * rows :] = tile.astype(jnp.float32).astype(jnp.bfloat16)
     b_ref[2 * heads * rows :] = tile.astype(jnp.float32).astype(jnp.bfloat16)
     for c in copies:
         c.wait()
@@ -67,7 +62,6 @@
         self.a, self.b = a_refs, b_refs
         self.scale = 1.0 / math.sqrt(self.width)
         self.rate = self.scale * LOG2E
-        self.key_heads = [self.head(x) for x in a_refs]
         self.query_heads = [self.head(x) for x in b_refs]
 
     def part(self, refs, index, group):
@@ -86,18 +80,18 @@
     def g(self, h, group):
         return self.part(self.b, self.heads + h, group)
 
-    def key_ids(self, group):
-        height = len(group) * self.blocks
-        row = lax.broadcasted_iota(jnp.int32, (height, self.rows), 0).astype(jnp.float32)
-        base = self.heads * self.slots
-        nk = jnp.zeros((height, self.rows), jnp.float32)
-        for i, s in enumerate(group):
-            first = self.key_heads[s][base : base + 1, 0:1] - i * self.blocks
-            nk = jnp.where(row >= i * self.blocks, row + first, nk)
-        seen = jnp.zeros((height, self.rows), jnp.float32)
+    def key_ids(self, distances):
+        shape = (len(distances) * self.blocks, self.rows)
+        row = lax.broadcasted_iota(jnp.int32, shape, 0)
+        me = lax.axis_index("seq")
+        nk = jnp.zeros(shape, jnp.int32)
+        for i, m in enumerate(distances):
+            nk = jnp.where(row >= i * self.blocks, row + ((me ^ m) - i) * self.blocks, nk)
+        nk = nk.astype(jnp.float32)
+        seen = jnp.zeros(shape, jnp.float32)
+        first = self.heads * self.slots + 1
         for n in range(self.gids):
-            gid = self.key_heads[group[0]][base + 1 + n : base + 2 + n]
-            seen = seen + jnp.where(nk == gid, 1.0, 0.0)
+            seen = seen + jnp.where(nk == self.query_heads[0][first + n : first + n + 1], 1.0, 0.0)
         return nk, seen
 
     def head(self, ref):
@@ -110,7 +104,7 @@
             cols = []
             for s in group:
                 head = self.query_heads[s]
-                nq = head[self.heads * self.slots :][:1]
+                nq = head[self.heads * self.slots : self.heads * self.slots + 1]
                 count = seen + jnp.where(jnp.abs(nk - nq) <= 1.0, 1.0, 0.0)
                 for j in range(self.slots):
                     r = h * self.slots + j
@@ -153,13 +147,14 @@
         return top, acc_l, acc_d
 
 
-def stats_kernel(sizes, n_keys, n_queries, *refs):
+def stats_kernel(sizes, distances, n_queries, *refs):
+    n_keys = len(distances)
     a_refs, b_refs = refs[:n_keys], refs[n_keys : n_keys + n_queries]
     before = refs[n_keys + n_queries : -3]
     stat, e_ref, dp_ref = refs[-3:]
     sh = Shards(sizes, a_refs, b_refs)
     keys, queries = list(range(n_keys)), list(range(n_queries))
-    bias = sh.bias(sh.key_ids(keys), queries)
+    bias = sh.bias(sh.key_ids(distances), queries)
     scored = [sh.scores(h, keys, queries) for h in range(sh.heads)]
     for h in range(sh.heads):
 
@@ -315,9 +310,13 @@
     vmem = pl.BlockSpec(memory_space=pltpu.VMEM)
     anyspace = pl.BlockSpec(memory_space=pl.ANY)
     params = pltpu.CompilerParams(vmem_limit_bytes=KERNEL_VMEM)
+    head_rows = -(-(heads * slots + 1 + global_ids.shape[0]) // 16) * 16
     a, b = pl.pallas_call(
         functools.partial(pack_kernel, sizes),
-        out_shape=(pltpu.VMEM((2 * heads * rows + head_rows, width), queries.dtype),) * 2,
+        out_shape=(
+            pltpu.VMEM((2 * heads * rows, width), queries.dtype),
+            pltpu.VMEM((2 * heads * rows + head_rows, width), queries.dtype),
+        ),
         in_specs=[anyspace] * 6,
         out_specs=(vmem, vmem),
         scratch_shapes=[
@@ -335,14 +334,16 @@
     a_all = [a_all[m] for m in range(n_keys)]
     lanes = n_queries * rows
     stat_rows = -(-3 * heads // 8) * 8
-    a_all = near([a_all[0]] + [a_all[m] for moves in key_moves(n_keys) for m in sorted(m for m, _ in moves)])
+    order = [0] + [m for moves in key_moves(n_keys) for m in sorted(m for m, _ in moves)]
+    a_all = near([a_all[m] for m in order])
     b_all = near(b_all)
     n_first = 1 + len(key_moves(n_keys)[0])
     stat, kept = None, []
-    for part in (a_all[:n_first], a_all[n_first:]):
+    for here in (slice(0, n_first), slice(n_first, n_keys)):
+        part = a_all[here]
         before = near([stat]) if kept else []
         stat, e, dp = pl.pallas_call(
-            functools.partial(stats_kernel, sizes, len(part), n_queries),
+            functools.partial(stats_kernel, sizes, order[here], n_queries),
             out_shape=(pltpu.VMEM((stat_rows, lanes), jnp.float32),)
             + (pltpu.VMEM((heads, len(part) * rows, lanes), jnp.float32),) * 2,
             compiler_params=params,
@@ -369,8 +370,7 @@
         in_specs=[vmem] * (2 * n_queries + 5),
         out_specs=(vmem,) * len(shapes),
     )(*b_all, *near(stats), *kept)
-    order = [m for moves in key_moves(n_keys) for m in sorted(m for m, _ in moves)]
-    parts = [parts[0]] + [exchanged(x, m) for m, x in zip(order, parts[1:])]
+    parts = [parts[0]] + [exchanged(x, m) for m, x in zip(order[1:], parts[1:])]
     out = jax.ShapeDtypeStruct(queries.shape, queries.dtype)
     grad_queries = pl.pallas_call(
         functools.partial(queries_kernel, sizes, widths),

time: 30.2 us -> 30 us (level)
  transfers between devices with their start and end apart: 9 -> 9, of which waited for: 7 -> 8; matrix products, arithmetic and copies ran while one was open for 0% -> 0% of each run, Pallas kernels for 8% -> 8%
where the time goes in v2:
time: 30 us; the launch traced here: 29.8 us
  starting transfers between devices  15.7 us (52%)
  waiting for transfers between devices  9.18 us (31%)
  Pallas kernels  4.25 us (14%)
  between operations  0.67 us (2%)
    ppermute x9, starting transfers between devices, exchanged(): lax.ppermute(value, 'seq', [(i, i ^ mask) for i in range(lax.axis_size('s...  15.7 us
    ppermute x9, waiting for transfers between devices, exchanged(): lax.ppermute(value, 'seq', [(i, i ^ mask) for i in range(lax.axis_size('s...  9.18 us
    pallas_call x1, Pallas kernels, gathered(): pl.pallas_call(functools.partial(queries_kernel, sizes, widths), out_shap...  0.96 us
    pallas_call x1, Pallas kernels, gathered(): pl.pallas_call(functools.partial(pack_kernel, sizes), out_shape=(pltpu.VM...  0.96 us
    pallas_call x2, Pallas kernels, gathered(): pl.pallas_call(functools.partial(stats_kernel, sizes, order[here], n_quer...  0.79 us
    pallas_call x1, Pallas kernels, gathered(): pl.pallas_call(functools.partial(sum_kernel, sizes, n_keys), out_shape=(o...  0.71 us
  transfers between devices with their start and end apart: 9, of which 8 were waited for; matrix products, arithmetic and copies ran while one was open for 0% of the time, Pallas kernels for 8%

profile of v2, /device:TPU:0, one launch (start us, length us, event | category | flops | bytes accessed | tf_op | source)
XLA Modules:
  0.0 29.8 jit_solution(773039423149486594)
XLA Ops:
  0.6 1.0 %shard_map.85 = (bf16[512,128]{1,0:T(8,128)(2,1)S(1)}, bf16[528,128]{1,0:T(8,128)(2,1)S(1)}) custom-call(s32[2,2,3]{2,1,0:T(2,128)} %ids_hbm.1, s32[2]{0:T(128)} %gids_hbm.1, bf16[2,128,128]{2,1,0:T(8,128)(2,1)} %k_ref.1, bf16[2,128,128]{2,1,0:T(8,128)(2,1)} %v_ref.1, bf16[2,128,128]{2,1,0:T(8,128)(2,1)} %q_ref.1, bf16[2,128,128]{2,1,0:T(8,128)(2,1)} %g_ref.1), custom_call_target="tpu_custom_call" | custom-call | tf_op jit(solution)/shard_map/pallas_call | solution.py:314
  1.6 3.1 %collective-permute-start.1 = (bf16[512,128]{1,0:T(8,128)(2,1)S(1)}, bf16[512,128]{1,0:T(8,128)(2,1)S(1)}, u32[]{:S(2)}, u32[]{:S(2)}) collective-permute-start(bf16[512,128]{1,0:T(8,128)(2,1)S(1)} %get-tuple-element.17.refs_0_), channel_id=1, source_target_pairs={{0,8},{4,12},{8,0},{12,4},{16,24},{20,28},{24,16},{28,20},{1,9},{5... | collective-permute-start | bytes 393224 | tf_op jit(solution)/shard_map/ppermute | solution.py:292
  4.7 2.6 %collective-permute-start.3 = (bf16[528,128]{1,0:T(8,128)(2,1)S(1)}, bf16[528,128]{1,0:T(8,128)(2,1)S(1)}, u32[]{:S(2)}, u32[]{:S(2)}) collective-permute-start(bf16[528,128]{1,0:T(8,128)(2,1)S(1)} %get-tuple-element.18.refs_3_.refs_1_.refs_0_), channel_id=1, source_target_pairs={{0,16},{4,20},{8,24},{12,28},{16,0},{20,4},{24,8},{28,12},{1,17},{... | collective-permute-start | bytes 405512 | tf_op jit(solution)/shard_map/ppermute | solution.py:292
  7.3 1.5 %collective-permute-start = (bf16[512,128]{1,0:T(8,128)(2,1)S(1)}, bf16[512,128]{1,0:T(8,128)(2,1)S(1)}, u32[]{:S(2)}, u32[]{:S(2)}) collective-permute-start(bf16[512,128]{1,0:T(8,128)(2,1)S(1)} %get-tuple-element.17.refs_0_), channel_id=1, source_target_pairs={{0,4},{4,0},{8,12},{12,8},{16,20},{20,16},{24,28},{28,24},{1,5},{5... | collective-permute-start | bytes 393224 | tf_op jit(solution)/shard_map/ppermute | solution.py:292
  8.8 1.2 %collective-permute-done.1.refs_2_ = bf16[512,128]{1,0:T(8,128)(2,1)S(1)} collective-permute-done((bf16[512,128]{1,0:T(8,128)(2,1)S(1)}, bf16[512,128]{1,0:T(8,128)(2,1)S(1)}, u32[]{:S(2)}, u32[]{:S(2)}) %collective-permute-start.1) | collective-permute-done | bytes 131104 | tf_op jit(solution)/shard_map/ppermute | solution.py:292
  10.1 1.8 %collective-permute-start.2 = (bf16[512,128]{1,0:T(8,128)(2,1)S(1)}, bf16[512,128]{1,0:T(8,128)(2,1)S(1)}, u32[]{:S(2)}, u32[]{:S(2)}) collective-permute-start(bf16[512,128]{1,0:T(8,128)(2,1)S(1)} %collective-permute-done.1.refs_2_), channel_id=1, source_target_pairs={{0,4},{4,0},{8,12},{12,8},{16,20},{20,16},{24,28},{28,24},{1,5},{5... | collective-permute-start | bytes 393224 | tf_op jit(solution)/shard_map/ppermute | solution.py:292
  11.9 1.5 %collective-permute-done.refs_1_ = bf16[512,128]{1,0:T(8,128)(2,1)S(1)} collective-permute-done((bf16[512,128]{1,0:T(8,128)(2,1)S(1)}, bf16[512,128]{1,0:T(8,128)(2,1)S(1)}, u32[]{:S(2)}, u32[]{:S(2)}) %collective-permute-start) | collective-permute-done | bytes 131104 | tf_op jit(solution)/shard_map/ppermute | solution.py:292
  13.4 0.2 collective-permute-done.3.refs_4_.refs_2_.refs_1_
  13.6 0.5 %shard_map.86 = (f32[8,256]{1,0:T(8,128)S(1)}, f32[2,384,256]{2,1,0:T(8,128)S(1)}, f32[2,384,256]{2,1,0:T(8,128)S(1)}) custom-call(bf16[512,128]{1,0:T(8,128)(2,1)S(1)} %get-tuple-element.17.refs_0_, bf16[512,128]{1,0:T(8,128)(2,1)S(1)} %collective-permute-done.refs_1_, bf16[512,128]{1,0:T(8,128)(2,1)S(1)} %collective-permute-done.1.refs_2_, ...), custom_call_target="tpu_custom_call" | custom-call | tf_op jit(solution)/shard_map/pallas_call | solution.py:345
  14.1 0.9 %collective-permute-done.2.refs_0_.refs_3_ = bf16[512,128]{1,0:T(8,128)(2,1)S(1)} collective-permute-done((bf16[512,128]{1,0:T(8,128)(2,1)S(1)}, bf16[512,128]{1,0:T(8,128)(2,1)S(1)}, u32[]{:S(2)}, u32[]{:S(2)}) %collective-permute-start.2) | collective-permute-done | bytes 131104 | tf_op jit(solution)/shard_map/ppermute | solution.py:292
  15.0 0.3 %shard_map.87 = (f32[8,256]{1,0:T(8,128)S(1)}, f32[2,128,256]{2,1,0:T(8,128)S(1)}, f32[2,128,256]{2,1,0:T(8,128)S(1)}) custom-call(bf16[512,128]{1,0:T(8,128)(2,1)S(1)} %collective-permute-done.2.refs_0_.refs_3_, bf16[528,128]{1,0:T(8,128)(2,1)S(1)} %get-tuple-element.18.refs_3_.refs_1_.refs_0_, ...), custom_call_target="tpu_custom_call" | custom-call | tf_op jit(solution)/shard_map/pallas_call | solution.py:345
  15.3 2.1 %collective-permute-start.4 = (f32[8,256]{1,0:T(8,128)S(1)}, f32[8,256]{1,0:T(8,128)S(1)}, u32[]{:S(2)}, u32[]{:S(2)}) collective-permute-start(f32[8,256]{1,0:T(8,128)S(1)} %get-tuple-element.20.refs_4_.refs_2_), channel_id=1, source_target_pairs={{0,16},{4,20},{8,24},{12,28},{16,0},{20,4},{24,8},{28,12},{1,17},{... | collective-permute-start | bytes 24584 | tf_op jit(solution)/shard_map/ppermute | solution.py:292
  17.4 0.4 %shard_map.88 = bf16[512,128]{1,0:T(8,128)(2,1)S(1)} custom-call(bf16[512,128]{1,0:T(8,128)(2,1)S(1)} %get-tuple-element.17.refs_0_, bf16[512,128]{1,0:T(8,128)(2,1)S(1)} %collective-permute-done.refs_1_, bf16[512,128]{1,0:T(8,128)(2,1)S(1)} %collective-permute-done.1.refs_2_, bf16[512,128]{1,0:T(8,128)(2,1)S(1)} %collective-permute-done.2.refs_0_.refs_3_, ...), custom_call_target="tpu_custom_call" | custom-call | tf_op jit(solution)/shard_map/pallas_call | solution.py:356
  17.8 1.0 %collective-permute-start.5 = (bf16[512,128]{1,0:T(8,128)(2,1)S(1)}, bf16[512,128]{1,0:T(8,128)(2,1)S(1)}, u32[]{:S(2)}, u32[]{:S(2)}) collective-permute-start(bf16[512,128]{1,0:T(8,128)(2,1)S(1)} %shard_map.88), channel_id=1, source_target_pairs={{0,16},{4,20},{8,24},{12,28},{16,0},{20,4},{24,8},{28,12},{1,17},{... | collective-permute-start | bytes 393224 | tf_op jit(solution)/shard_map/ppermute | solution.py:292
  18.8 1.2 %collective-permute-done.4.refs_5_.refs_3_ = f32[8,256]{1,0:T(8,128)S(1)} collective-permute-done((f32[8,256]{1,0:T(8,128)S(1)}, f32[8,256]{1,0:T(8,128)S(1)}, u32[]{:S(2)}, u32[]{:S(2)}) %collective-permute-start.4) | collective-permute-done | bytes 8224 | tf_op jit(solution)/shard_map/ppermute | solution.py:292
  20.0 0.4 %shard_map.90 = (f32[512,128]{1,0:T(8,128)S(1)}, bf16[512,128]{1,0:T(8,128)(2,1)S(1)}, bf16[512,128]{1,0:T(8,128)(2,1)S(1)}, bf16[512,128]{1,0:T(8,128)(2,1)S(1)}) custom-call(bf16[528,128]{1,0:T(8,128)(2,1)S(1)} %get-tuple-element.18.refs_3_.refs_1_.refs_0_, bf16[528,128]{1,0:T(8,128)(2,1)S(1)} %collective-permute-done.3.refs_4_.refs_2_.refs_1_, ...), custom_call_target="tpu_custom_call" | custom-call | tf_op jit(solution)/shard_map/pallas_call | solution.py:366
  20.4 1.9 %collective-permute-start.6 = (bf16[512,128]{1,0:T(8,128)(2,1)S(1)}, bf16[512,128]{1,0:T(8,128)(2,1)S(1)}, u32[]{:S(2)}, u32[]{:S(2)}) collective-permute-start(bf16[512,128]{1,0:T(8,128)(2,1)S(1)} %get-tuple-element.26), channel_id=1, source_target_pairs={{0,4},{4,0},{8,12},{12,8},{16,20},{20,16},{24,28},{28,24},{1,5},{5... | collective-permute-start | bytes 393224 | tf_op jit(solution)/shard_map/ppermute | solution.py:292
  22.3 0.9 %collective-permute-start.7 = (bf16[512,128]{1,0:T(8,128)(2,1)S(1)}, bf16[512,128]{1,0:T(8,128)(2,1)S(1)}, u32[]{:S(2)}, u32[]{:S(2)}) collective-permute-start(bf16[512,128]{1,0:T(8,128)(2,1)S(1)} %get-tuple-element.27), channel_id=1, source_target_pairs={{0,8},{4,12},{8,0},{12,4},{16,24},{20,28},{24,16},{28,20},{1,9},{5... | collective-permute-start | bytes 393224 | tf_op jit(solution)/shard_map/ppermute | solution.py:292
  23.2 0.8 %collective-permute-start.8 = (bf16[512,128]{1,0:T(8,128)(2,1)S(1)}, bf16[512,128]{1,0:T(8,128)(2,1)S(1)}, u32[]{:S(2)}, u32[]{:S(2)}) collective-permute-start(bf16[512,128]{1,0:T(8,128)(2,1)S(1)} %get-tuple-element.28), channel_id=1, source_target_pairs={{0,12},{4,8},{8,4},{12,0},{16,28},{20,24},{24,20},{28,16},{1,13},{... | collective-permute-start | bytes 393224 | tf_op jit(solution)/shard_map/ppermute | solution.py:292
  24.0 0.0 collective-permute-done.5.refs_11_
  24.0 1.0 %shard_map.89 = bf16[2,128,128]{2,1,0:T(8,128)(2,1)} custom-call(bf16[512,128]{1,0:T(8,128)(2,1)S(1)} %get-tuple-element.17.refs_0_, bf16[512,128]{1,0:T(8,128)(2,1)S(1)} %collective-permute-done.refs_1_, bf16[512,128]{1,0:T(8,128)(2,1)S(1)} %collective-permute-done.1.refs_2_, bf16[512,128]{1,0:T(8,128)(2,1)S(1)} %collective-permute-done.2.refs_0_.refs_3_, ...), custom_call_target="tpu_custom_call" | custom-call | tf_op jit(solution)/shard_map/pallas_call | solution.py:375
  24.9 1.6 %collective-permute-done.6.refs_1_ = bf16[512,128]{1,0:T(8,128)(2,1)S(1)} collective-permute-done((bf16[512,128]{1,0:T(8,128)(2,1)S(1)}, bf16[512,128]{1,0:T(8,128)(2,1)S(1)}, u32[]{:S(2)}, u32[]{:S(2)}) %collective-permute-start.6) | collective-permute-done | bytes 131104 | tf_op jit(solution)/shard_map/ppermute | solution.py:292
  26.5 0.8 %collective-permute-done.7.refs_2_ = bf16[512,128]{1,0:T(8,128)(2,1)S(1)} collective-permute-done((bf16[512,128]{1,0:T(8,128)(2,1)S(1)}, bf16[512,128]{1,0:T(8,128)(2,1)S(1)}, u32[]{:S(2)}, u32[]{:S(2)}) %collective-permute-start.7) | collective-permute-done | bytes 131104 | tf_op jit(solution)/shard_map/ppermute | solution.py:292
  27.3 1.8 %collective-permute-done.8.refs_3_ = bf16[512,128]{1,0:T(8,128)(2,1)S(1)} collective-permute-done((bf16[512,128]{1,0:T(8,128)(2,1)S(1)}, bf16[512,128]{1,0:T(8,128)(2,1)S(1)}, u32[]{:S(2)}, u32[]{:S(2)}) %collective-permute-start.8) | collective-permute-done | bytes 131104 | tf_op jit(solution)/shard_map/ppermute | solution.py:292
  29.1 0.7 %shard_map.91 = (bf16[2,128,128]{2,1,0:T(8,128)(2,1)}, bf16[2,128,128]{2,1,0:T(8,128)(2,1)}) custom-call(f32[512,128]{1,0:T(8,128)S(1)} %get-tuple-element.25.refs_0_, bf16[512,128]{1,0:T(8,128)(2,1)S(1)} %collective-permute-done.6.refs_1_, bf16[512,128]{1,0:T(8,128)(2,1)S(1)} %collective-permute-done.7.refs_2_, ...), custom_call_target="tpu_custom_call" | custom-call | tf_op jit(solution)/shard_map/pallas_call | solution.py:383
Async XLA Ops:
  1.6 8.5 %collective-permute-start.1 = (bf16[512,128]{1,0:T(8,128)(2,1)S(1)}, bf16[512,128]{1,0:T(8,128)(2,1)S(1)}, u32[]{:S(2)}, u32[]{:S(2)}) collective-permute-start(bf16[512,128]{1,0:T(8,128)(2,1)S(1)} %get-tuple-element.17.refs_0_), channel_id=1, source_target_pairs={{0,8},{4,12},{8,0},{12,4},{16,24},{20,28},{24,16},{28,20},{1,9},{5... | collective-permute-start | bytes 393224 | tf_op jit(solution)/shard_map/ppermute | solution.py:292
  4.7 8.9 %collective-permute-start.3 = (bf16[528,128]{1,0:T(8,128)(2,1)S(1)}, bf16[528,128]{1,0:T(8,128)(2,1)S(1)}, u32[]{:S(2)}, u32[]{:S(2)}) collective-permute-start(bf16[528,128]{1,0:T(8,128)(2,1)S(1)} %get-tuple-element.18.refs_3_.refs_1_.refs_0_), channel_id=1, source_target_pairs={{0,16},{4,20},{8,24},{12,28},{16,0},{20,4},{24,8},{28,12},{1,17},{... | collective-permute-start | bytes 405512 | tf_op jit(solution)/shard_map/ppermute | solution.py:292
  7.3 6.1 %collective-permute-start = (bf16[512,128]{1,0:T(8,128)(2,1)S(1)}, bf16[512,128]{1,0:T(8,128)(2,1)S(1)}, u32[]{:S(2)}, u32[]{:S(2)}) collective-permute-start(bf16[512,128]{1,0:T(8,128)(2,1)S(1)} %get-tuple-element.17.refs_0_), channel_id=1, source_target_pairs={{0,4},{4,0},{8,12},{12,8},{16,20},{20,16},{24,28},{28,24},{1,5},{5... | collective-permute-start | bytes 393224 | tf_op jit(solution)/shard_map/ppermute | solution.py:292
  10.1 5.0 %collective-permute-start.2 = (bf16[512,128]{1,0:T(8,128)(2,1)S(1)}, bf16[512,128]{1,0:T(8,128)(2,1)S(1)}, u32[]{:S(2)}, u32[]{:S(2)}) collective-permute-start(bf16[512,128]{1,0:T(8,128)(2,1)S(1)} %collective-permute-done.1.refs_2_), channel_id=1, source_target_pairs={{0,4},{4,0},{8,12},{12,8},{16,20},{20,16},{24,28},{28,24},{1,5},{5... | collective-permute-start | bytes 393224 | tf_op jit(solution)/shard_map/ppermute | solution.py:292
  15.3 4.6 %collective-permute-start.4 = (f32[8,256]{1,0:T(8,128)S(1)}, f32[8,256]{1,0:T(8,128)S(1)}, u32[]{:S(2)}, u32[]{:S(2)}) collective-permute-start(f32[8,256]{1,0:T(8,128)S(1)} %get-tuple-element.20.refs_4_.refs_2_), channel_id=1, source_target_pairs={{0,16},{4,20},{8,24},{12,28},{16,0},{20,4},{24,8},{28,12},{1,17},{... | collective-permute-start | bytes 24584 | tf_op jit(solution)/shard_map/ppermute | solution.py:292
  17.8 6.2 %collective-permute-start.5 = (bf16[512,128]{1,0:T(8,128)(2,1)S(1)}, bf16[512,128]{1,0:T(8,128)(2,1)S(1)}, u32[]{:S(2)}, u32[]{:S(2)}) collective-permute-start(bf16[512,128]{1,0:T(8,128)(2,1)S(1)} %shard_map.88), channel_id=1, source_target_pairs={{0,16},{4,20},{8,24},{12,28},{16,0},{20,4},{24,8},{28,12},{1,17},{... | collective-permute-start | bytes 393224 | tf_op jit(solution)/shard_map/ppermute | solution.py:292
  20.4 6.1 %collective-permute-start.6 = (bf16[512,128]{1,0:T(8,128)(2,1)S(1)}, bf16[512,128]{1,0:T(8,128)(2,1)S(1)}, u32[]{:S(2)}, u32[]{:S(2)}) collective-permute-start(bf16[512,128]{1,0:T(8,128)(2,1)S(1)} %get-tuple-element.26), channel_id=1, source_target_pairs={{0,4},{4,0},{8,12},{12,8},{16,20},{20,16},{24,28},{28,24},{1,5},{5... | collective-permute-start | bytes 393224 | tf_op jit(solution)/shard_map/ppermute | solution.py:292
  22.3 5.0 %collective-permute-start.7 = (bf16[512,128]{1,0:T(8,128)(2,1)S(1)}, bf16[512,128]{1,0:T(8,128)(2,1)S(1)}, u32[]{:S(2)}, u32[]{:S(2)}) collective-permute-start(bf16[512,128]{1,0:T(8,128)(2,1)S(1)} %get-tuple-element.27), channel_id=1, source_target_pairs={{0,8},{4,12},{8,0},{12,4},{16,24},{20,28},{24,16},{28,20},{1,9},{5... | collective-permute-start | bytes 393224 | tf_op jit(solution)/shard_map/ppermute | solution.py:292
  23.2 5.9 %collective-permute-start.8 = (bf16[512,128]{1,0:T(8,128)(2,1)S(1)}, bf16[512,128]{1,0:T(8,128)(2,1)S(1)}, u32[]{:S(2)}, u32[]{:S(2)}) collective-permute-start(bf16[512,128]{1,0:T(8,128)(2,1)S(1)} %get-tuple-element.28), channel_id=1, source_target_pairs={{0,12},{4,8},{8,4},{12,0},{16,28},{20,24},{24,20},{28,16},{1,13},{... | collective-permute-start | bytes 393224 | tf_op jit(solution)/shard_map/ppermute | solution.py:292

commit v3 on v2

--- a/solution.py
+++ b/solution.py
@@ -219,9 +219,9 @@
     return top + jnp.log2(total), weighted / total
 
 
-def grads_kernel(sizes, widths, *refs):
+def grads_kernel(sizes, widths, picked, *refs):
     heads, rows = sizes[0], sizes[2]
-    n_keys, n_queries = widths
+    _, n_queries = widths
     b_refs = refs[:n_queries]
     stats, kept = refs[n_queries : 2 * n_queries], refs[2 * n_queries : 2 * n_queries + 5]
     kv_out = refs[2 * n_queries + 5 :]
@@ -231,12 +231,13 @@
         whole = [whole_stats(stats, rows, h, s) for s in queries]
         shift, dots = (jnp.concatenate([x[i] for x in whole], axis=1) for i in range(2))
         p_low, ds_low = [], []
-        for p, dp in kept_tiles(sh, kept, stats[0], h, slice(0, n_queries * rows), shift):
+        tiles = list(kept_tiles(sh, kept, stats[0], h, slice(0, n_queries * rows), shift))
+        for p, dp in tiles[picked.start * sh.blocks : picked.stop * sh.blocks]:
             p_low.append(p.astype(jnp.bfloat16))
             ds_low.append((p * (dp - dots)).astype(jnp.bfloat16))
         dk = jnp.dot(jnp.concatenate(ds_low), sh.q(h, queries), preferred_element_type=jnp.float32) * sh.scale
         dv = jnp.dot(jnp.concatenate(p_low), sh.g(h, queries), preferred_element_type=jnp.float32)
-        for m in range(n_keys):
+        for m in range(len(kv_out)):
             cut = slice(m * rows, (m + 1) * rows)
             kv_out[m][h * rows : (h + 1) * rows] = dk[cut].astype(kv_out[m].dtype)
             kv_out[m][(heads + h) * rows : (heads + h + 1) * rows] = dv[cut].astype(kv_out[m].dtype)
@@ -278,8 +279,8 @@
             cut = slice((i * heads + h) * rows, (i * heads + h + 1) * rows)
             total = sum(p[cut].astype(jnp.float32) for p in parts)
             bufs[i][h] = total.astype(bufs[i].dtype)
-        copies.append(pltpu.make_async_copy(bufs[i], outs[i], sems.at[i]))
-        copies[-1].start()
+            copies.append(pltpu.make_async_copy(bufs[i].at[h], outs[i].at[h], sems.at[i * heads + h]))
+            copies[-1].start()
     for c in copies:
         c.wait()
 
@@ -363,13 +364,16 @@
     sums = [exchanged(x, s * n_keys) for s, x in zip(range(1, n_queries), sums)]
     shapes = [pltpu.VMEM((2 * heads * rows, width), jnp.float32)]
     shapes += [pltpu.VMEM((2 * heads * rows, width), queries.dtype)] * (n_keys - 1)
-    parts = pl.pallas_call(
-        functools.partial(grads_kernel, sizes, widths),
-        out_shape=tuple(shapes),
-        compiler_params=params,
-        in_specs=[vmem] * (2 * n_queries + 5),
-        out_specs=(vmem,) * len(shapes),
-    )(*b_all, *near(stats), *kept)
+    parts = []
+    for picked in (slice(n_first, n_keys), slice(0, n_first)):
+        got = pl.pallas_call(
+            functools.partial(grads_kernel, sizes, widths, picked),
+            out_shape=tuple(shapes[picked]),
+            compiler_params=params,
+            in_specs=[vmem] * (2 * n_queries + 5),
+            out_specs=(vmem,) * len(shapes[picked]),
+        )(*b_all, *near(stats), *kept)
+        parts = [*got, *parts]
     parts = [parts[0]] + [exchanged(x, m) for m, x in zip(order[1:], parts[1:])]
     out = jax.ShapeDtypeStruct(queries.shape, queries.dtype)
     grad_queries = pl.pallas_call(
@@ -386,7 +390,7 @@
         compiler_params=params,
         in_specs=[vmem] * n_keys,
         out_specs=(anyspace,) * 2,
-        scratch_shapes=[buf, buf, pltpu.SemaphoreType.DMA((2,))],
+        scratch_shapes=[buf, buf, pltpu.SemaphoreType.DMA((2 * heads,))],
     )(*near(parts))
     return grad_queries, grad_keys, grad_values
 

time: 30 us -> 30.2 us (level)
    pallas_call x1 -> x2, Pallas kernels: 0.45 us -> 0.63 us  [gathered(): pl.pallas_call(functools.partial(grads_kernel, sizes, widths, picked), ou...]
where the time goes in v3:
time: 30.2 us; the launch traced here: 30 us
  starting transfers between devices  15.8 us (52%)
  waiting for transfers between devices  9.18 us (30%)
  Pallas kernels  4.44 us (15%)
  between operations  0.68 us (2%)
    ppermute x9, starting transfers between devices, exchanged(): lax.ppermute(value, 'seq', [(i, i ^ mask) for i in range(lax.axis_size('s...  15.8 us
    ppermute x9, waiting for transfers between devices, exchanged(): lax.ppermute(value, 'seq', [(i, i ^ mask) for i in range(lax.axis_size('s...  9.18 us
    pallas_call x1, Pallas kernels, gathered(): pl.pallas_call(functools.partial(queries_kernel, sizes, widths), out_shap...  0.96 us
    pallas_call x1, Pallas kernels, gathered(): pl.pallas_call(functools.partial(pack_kernel, sizes), out_shape=(pltpu.VM...  0.96 us
    pallas_call x2, Pallas kernels, gathered(): pl.pallas_call(functools.partial(stats_kernel, sizes, order[here], n_quer...  0.79 us
    pallas_call x1, Pallas kernels, gathered(): pl.pallas_call(functools.partial(sum_kernel, sizes, n_keys), out_shape=(o...  0.71 us
    pallas_call x2, Pallas kernels, gathered(): pl.pallas_call(functools.partial(grads_kernel, sizes, widths, picked), ou...  0.63 us
  transfers between devices with their start and end apart: 9, of which 8 were waited for; matrix products, arithmetic and copies ran while one was open for 0% of the time, Pallas kernels for 8%

profile of v3, /device:TPU:0, one launch (start us, length us, event | category | flops | bytes accessed | tf_op | source)
XLA Modules:
  0.0 30.0 jit_solution(6518464861071213012)
XLA Ops:
  0.6 1.0 %shard_map.85 = (bf16[512,128]{1,0:T(8,128)(2,1)S(1)}, bf16[528,128]{1,0:T(8,128)(2,1)S(1)}) custom-call(s32[2,2,3]{2,1,0:T(2,128)} %ids_hbm.1, s32[2]{0:T(128)} %gids_hbm.1, bf16[2,128,128]{2,1,0:T(8,128)(2,1)} %k_ref.1, bf16[2,128,128]{2,1,0:T(8,128)(2,1)} %v_ref.1, bf16[2,128,128]{2,1,0:T(8,128)(2,1)} %q_ref.1, bf16[2,128,128]{2,1,0:T(8,128)(2,1)} %g_ref.1), custom_call_target="tpu_custom_call" | custom-call | tf_op jit(solution)/shard_map/pallas_call | solution.py:315
  1.6 3.1 %collective-permute-start.1 = (bf16[512,128]{1,0:T(8,128)(2,1)S(1)}, bf16[512,128]{1,0:T(8,128)(2,1)S(1)}, u32[]{:S(2)}, u32[]{:S(2)}) collective-permute-start(bf16[512,128]{1,0:T(8,128)(2,1)S(1)} %get-tuple-element.16.refs_0_), channel_id=1, source_target_pairs={{0,8},{4,12},{8,0},{12,4},{16,24},{20,28},{24,16},{28,20},{1,9},{5... | collective-permute-start | bytes 393224 | tf_op jit(solution)/shard_map/ppermute | solution.py:293
  4.7 2.6 %collective-permute-start.3 = (bf16[528,128]{1,0:T(8,128)(2,1)S(1)}, bf16[528,128]{1,0:T(8,128)(2,1)S(1)}, u32[]{:S(2)}, u32[]{:S(2)}) collective-permute-start(bf16[528,128]{1,0:T(8,128)(2,1)S(1)} %get-tuple-element.17.refs_3_.refs_1_.refs_0_), channel_id=1, source_target_pairs={{0,16},{4,20},{8,24},{12,28},{16,0},{20,4},{24,8},{28,12},{1,17},{... | collective-permute-start | bytes 405512 | tf_op jit(solution)/shard_map/ppermute | solution.py:293
  7.3 1.5 %collective-permute-start = (bf16[512,128]{1,0:T(8,128)(2,1)S(1)}, bf16[512,128]{1,0:T(8,128)(2,1)S(1)}, u32[]{:S(2)}, u32[]{:S(2)}) collective-permute-start(bf16[512,128]{1,0:T(8,128)(2,1)S(1)} %get-tuple-element.16.refs_0_), channel_id=1, source_target_pairs={{0,4},{4,0},{8,12},{12,8},{16,20},{20,16},{24,28},{28,24},{1,5},{5... | collective-permute-start | bytes 393224 | tf_op jit(solution)/shard_map/ppermute | solution.py:293
  8.8 1.2 %collective-permute-done.1.refs_2_ = bf16[512,128]{1,0:T(8,128)(2,1)S(1)} collective-permute-done((bf16[512,128]{1,0:T(8,128)(2,1)S(1)}, bf16[512,128]{1,0:T(8,128)(2,1)S(1)}, u32[]{:S(2)}, u32[]{:S(2)}) %collective-permute-start.1) | collective-permute-done | bytes 131104 | tf_op jit(solution)/shard_map/ppermute | solution.py:293
  10.1 1.8 %collective-permute-start.2 = (bf16[512,128]{1,0:T(8,128)(2,1)S(1)}, bf16[512,128]{1,0:T(8,128)(2,1)S(1)}, u32[]{:S(2)}, u32[]{:S(2)}) collective-permute-start(bf16[512,128]{1,0:T(8,128)(2,1)S(1)} %collective-permute-done.1.refs_2_), channel_id=1, source_target_pairs={{0,4},{4,0},{8,12},{12,8},{16,20},{20,16},{24,28},{28,24},{1,5},{5... | collective-permute-start | bytes 393224 | tf_op jit(solution)/shard_map/ppermute | solution.py:293
  11.9 1.5 %collective-permute-done.refs_1_ = bf16[512,128]{1,0:T(8,128)(2,1)S(1)} collective-permute-done((bf16[512,128]{1,0:T(8,128)(2,1)S(1)}, bf16[512,128]{1,0:T(8,128)(2,1)S(1)}, u32[]{:S(2)}, u32[]{:S(2)}) %collective-permute-start) | collective-permute-done | bytes 131104 | tf_op jit(solution)/shard_map/ppermute | solution.py:293
  13.4 0.2 collective-permute-done.3.refs_4_.refs_2_.refs_1_
  13.6 0.5 %shard_map.86 = (f32[8,256]{1,0:T(8,128)S(1)}, f32[2,384,256]{2,1,0:T(8,128)S(1)}, f32[2,384,256]{2,1,0:T(8,128)S(1)}) custom-call(bf16[512,128]{1,0:T(8,128)(2,1)S(1)} %get-tuple-element.16.refs_0_, bf16[512,128]{1,0:T(8,128)(2,1)S(1)} %collective-permute-done.refs_1_, bf16[512,128]{1,0:T(8,128)(2,1)S(1)} %collective-permute-done.1.refs_2_, ...), custom_call_target="tpu_custom_call" | custom-call | tf_op jit(solution)/shard_map/pallas_call | solution.py:346
  14.1 0.9 %collective-permute-done.2.refs_0_.refs_3_ = bf16[512,128]{1,0:T(8,128)(2,1)S(1)} collective-permute-done((bf16[512,128]{1,0:T(8,128)(2,1)S(1)}, bf16[512,128]{1,0:T(8,128)(2,1)S(1)}, u32[]{:S(2)}, u32[]{:S(2)}) %collective-permute-start.2) | collective-permute-done | bytes 131104 | tf_op jit(solution)/shard_map/ppermute | solution.py:293
  15.0 0.3 shard_map.87
  15.3 2.1 %collective-permute-start.4 = (f32[8,256]{1,0:T(8,128)S(1)}, f32[8,256]{1,0:T(8,128)S(1)}, u32[]{:S(2)}, u32[]{:S(2)}) collective-permute-start(f32[8,256]{1,0:T(8,128)S(1)} %get-tuple-element.19.refs_4_.refs_2_), channel_id=1, source_target_pairs={{0,16},{4,20},{8,24},{12,28},{16,0},{20,4},{24,8},{28,12},{1,17},{... | collective-permute-start | bytes 24584 | tf_op jit(solution)/shard_map/ppermute | solution.py:293
  17.4 0.4 %shard_map.88 = bf16[512,128]{1,0:T(8,128)(2,1)S(1)} custom-call(bf16[512,128]{1,0:T(8,128)(2,1)S(1)} %get-tuple-element.16.refs_0_, bf16[512,128]{1,0:T(8,128)(2,1)S(1)} %collective-permute-done.refs_1_, bf16[512,128]{1,0:T(8,128)(2,1)S(1)} %collective-permute-done.1.refs_2_, bf16[512,128]{1,0:T(8,128)(2,1)S(1)} %collective-permute-done.2.refs_0_.refs_3_, ...), custom_call_target="tpu_custom_call" | custom-call | tf_op jit(solution)/shard_map/pallas_call | solution.py:357
  17.8 1.0 %collective-permute-start.5 = (bf16[512,128]{1,0:T(8,128)(2,1)S(1)}, bf16[512,128]{1,0:T(8,128)(2,1)S(1)}, u32[]{:S(2)}, u32[]{:S(2)}) collective-permute-start(bf16[512,128]{1,0:T(8,128)(2,1)S(1)} %shard_map.88), channel_id=1, source_target_pairs={{0,16},{4,20},{8,24},{12,28},{16,0},{20,4},{24,8},{28,12},{1,17},{... | collective-permute-start | bytes 393224 | tf_op jit(solution)/shard_map/ppermute | solution.py:293
  18.8 1.2 %collective-permute-done.4.refs_5_.refs_3_ = f32[8,256]{1,0:T(8,128)S(1)} collective-permute-done((f32[8,256]{1,0:T(8,128)S(1)}, f32[8,256]{1,0:T(8,128)S(1)}, u32[]{:S(2)}, u32[]{:S(2)}) %collective-permute-start.4) | collective-permute-done | bytes 8224 | tf_op jit(solution)/shard_map/ppermute | solution.py:293
  20.0 0.4 %shard_map.90 = (f32[512,128]{1,0:T(8,128)S(1)}, bf16[512,128]{1,0:T(8,128)(2,1)S(1)}, bf16[512,128]{1,0:T(8,128)(2,1)S(1)}) custom-call(bf16[528,128]{1,0:T(8,128)(2,1)S(1)} %get-tuple-element.17.refs_3_.refs_1_.refs_0_, bf16[528,128]{1,0:T(8,128)(2,1)S(1)} %collective-permute-done.3.refs_4_.refs_2_.refs_1_, ...), custom_call_target="tpu_custom_call" | custom-call | tf_op jit(solution)/shard_map/pallas_call | solution.py:369
  20.3 1.9 %collective-permute-start.6 = (bf16[512,128]{1,0:T(8,128)(2,1)S(1)}, bf16[512,128]{1,0:T(8,128)(2,1)S(1)}, u32[]{:S(2)}, u32[]{:S(2)}) collective-permute-start(bf16[512,128]{1,0:T(8,128)(2,1)S(1)} %get-tuple-element.25), channel_id=1, source_target_pairs={{0,4},{4,0},{8,12},{12,8},{16,20},{20,16},{24,28},{28,24},{1,5},{5... | collective-permute-start | bytes 393224 | tf_op jit(solution)/shard_map/ppermute | solution.py:293
  22.3 0.9 %collective-permute-start.7 = (bf16[512,128]{1,0:T(8,128)(2,1)S(1)}, bf16[512,128]{1,0:T(8,128)(2,1)S(1)}, u32[]{:S(2)}, u32[]{:S(2)}) collective-permute-start(bf16[512,128]{1,0:T(8,128)(2,1)S(1)} %get-tuple-element.26), channel_id=1, source_target_pairs={{0,8},{4,12},{8,0},{12,4},{16,24},{20,28},{24,16},{28,20},{1,9},{5... | collective-permute-start | bytes 393224 | tf_op jit(solution)/shard_map/ppermute | solution.py:293
  23.1 0.3 shard_map.91
  23.4 0.8 %collective-permute-start.8 = (bf16[512,128]{1,0:T(8,128)(2,1)S(1)}, bf16[512,128]{1,0:T(8,128)(2,1)S(1)}, u32[]{:S(2)}, u32[]{:S(2)}) collective-permute-start(bf16[512,128]{1,0:T(8,128)(2,1)S(1)} %shard_map.91), channel_id=1, source_target_pairs={{0,12},{4,8},{8,4},{12,0},{16,28},{20,24},{24,20},{28,16},{1,13},{... | collective-permute-start | bytes 393224 | tf_op jit(solution)/shard_map/ppermute | solution.py:293
  24.2 0.0 collective-permute-done.5.refs_11_
  24.2 1.0 %shard_map.89 = bf16[2,128,128]{2,1,0:T(8,128)(2,1)} custom-call(bf16[512,128]{1,0:T(8,128)(2,1)S(1)} %get-tuple-element.16.refs_0_, bf16[512,128]{1,0:T(8,128)(2,1)S(1)} %collective-permute-done.refs_1_, bf16[512,128]{1,0:T(8,128)(2,1)S(1)} %collective-permute-done.1.refs_2_, bf16[512,128]{1,0:T(8,128)(2,1)S(1)} %collective-permute-done.2.refs_0_.refs_3_, ...), custom_call_target="tpu_custom_call" | custom-call | tf_op jit(solution)/shard_map/pallas_call | solution.py:379
  25.2 1.4 %collective-permute-done.6.refs_1_ = bf16[512,128]{1,0:T(8,128)(2,1)S(1)} collective-permute-done((bf16[512,128]{1,0:T(8,128)(2,1)S(1)}, bf16[512,128]{1,0:T(8,128)(2,1)S(1)}, u32[]{:S(2)}, u32[]{:S(2)}) %collective-permute-start.6) | collective-permute-done | bytes 131104 | tf_op jit(solution)/shard_map/ppermute | solution.py:293
  26.6 0.6 %collective-permute-done.7.refs_2_ = bf16[512,128]{1,0:T(8,128)(2,1)S(1)} collective-permute-done((bf16[512,128]{1,0:T(8,128)(2,1)S(1)}, bf16[512,128]{1,0:T(8,128)(2,1)S(1)}, u32[]{:S(2)}, u32[]{:S(2)}) %collective-permute-start.7) | collective-permute-done | bytes 131104 | tf_op jit(solution)/shard_map/ppermute | solution.py:293
  27.2 2.1 %collective-permute-done.8.refs_3_ = bf16[512,128]{1,0:T(8,128)(2,1)S(1)} collective-permute-done((bf16[512,128]{1,0:T(8,128)(2,1)S(1)}, bf16[512,128]{1,0:T(8,128)(2,1)S(1)}, u32[]{:S(2)}, u32[]{:S(2)}) %collective-permute-start.8) | collective-permute-done | bytes 131104 | tf_op jit(solution)/shard_map/ppermute | solution.py:293
  29.3 0.7 %shard_map.92 = (bf16[2,128,128]{2,1,0:T(8,128)(2,1)}, bf16[2,128,128]{2,1,0:T(8,128)(2,1)}) custom-call(f32[512,128]{1,0:T(8,128)S(1)} %get-tuple-element.24.refs_0_, bf16[512,128]{1,0:T(8,128)(2,1)S(1)} %collective-permute-done.6.refs_1_, bf16[512,128]{1,0:T(8,128)(2,1)S(1)} %collective-permute-done.7.refs_2_, ...), custom_call_target="tpu_custom_call" | custom-call | tf_op jit(solution)/shard_map/pallas_call | solution.py:387
Async XLA Ops:
  1.6 8.5 %collective-permute-start.1 = (bf16[512,128]{1,0:T(8,128)(2,1)S(1)}, bf16[512,128]{1,0:T(8,128)(2,1)S(1)}, u32[]{:S(2)}, u32[]{:S(2)}) collective-permute-start(bf16[512,128]{1,0:T(8,128)(2,1)S(1)} %get-tuple-element.16.refs_0_), channel_id=1, source_target_pairs={{0,8},{4,12},{8,0},{12,4},{16,24},{20,28},{24,16},{28,20},{1,9},{5... | collective-permute-start | bytes 393224 | tf_op jit(solution)/shard_map/ppermute | solution.py:293
  4.7 8.9 %collective-permute-start.3 = (bf16[528,128]{1,0:T(8,128)(2,1)S(1)}, bf16[528,128]{1,0:T(8,128)(2,1)S(1)}, u32[]{:S(2)}, u32[]{:S(2)}) collective-permute-start(bf16[528,128]{1,0:T(8,128)(2,1)S(1)} %get-tuple-element.17.refs_3_.refs_1_.refs_0_), channel_id=1, source_target_pairs={{0,16},{4,20},{8,24},{12,28},{16,0},{20,4},{24,8},{28,12},{1,17},{... | collective-permute-start | bytes 405512 | tf_op jit(solution)/shard_map/ppermute | solution.py:293
  7.3 6.1 %collective-permute-start = (bf16[512,128]{1,0:T(8,128)(2,1)S(1)}, bf16[512,128]{1,0:T(8,128)(2,1)S(1)}, u32[]{:S(2)}, u32[]{:S(2)}) collective-permute-start(bf16[512,128]{1,0:T(8,128)(2,1)S(1)} %get-tuple-element.16.refs_0_), channel_id=1, source_target_pairs={{0,4},{4,0},{8,12},{12,8},{16,20},{20,16},{24,28},{28,24},{1,5},{5... | collective-permute-start | bytes 393224 | tf_op jit(solution)/shard_map/ppermute | solution.py:293
  10.1 5.0 %collective-permute-start.2 = (bf16[512,128]{1,0:T(8,128)(2,1)S(1)}, bf16[512,128]{1,0:T(8,128)(2,1)S(1)}, u32[]{:S(2)}, u32[]{:S(2)}) collective-permute-start(bf16[512,128]{1,0:T(8,128)(2,1)S(1)} %collective-permute-done.1.refs_2_), channel_id=1, source_target_pairs={{0,4},{4,0},{8,12},{12,8},{16,20},{20,16},{24,28},{28,24},{1,5},{5... | collective-permute-start | bytes 393224 | tf_op jit(solution)/shard_map/ppermute | solution.py:293
  15.3 4.6 %collective-permute-start.4 = (f32[8,256]{1,0:T(8,128)S(1)}, f32[8,256]{1,0:T(8,128)S(1)}, u32[]{:S(2)}, u32[]{:S(2)}) collective-permute-start(f32[8,256]{1,0:T(8,128)S(1)} %get-tuple-element.19.refs_4_.refs_2_), channel_id=1, source_target_pairs={{0,16},{4,20},{8,24},{12,28},{16,0},{20,4},{24,8},{28,12},{1,17},{... | collective-permute-start | bytes 24584 | tf_op jit(solution)/shard_map/ppermute | solution.py:293
  17.8 6.4 %collective-permute-start.5 = (bf16[512,128]{1,0:T(8,128)(2,1)S(1)}, bf16[512,128]{1,0:T(8,128)(2,1)S(1)}, u32[]{:S(2)}, u32[]{:S(2)}) collective-permute-start(bf16[512,128]{1,0:T(8,128)(2,1)S(1)} %shard_map.88), channel_id=1, source_target_pairs={{0,16},{4,20},{8,24},{12,28},{16,0},{20,4},{24,8},{28,12},{1,17},{... | collective-permute-start | bytes 393224 | tf_op jit(solution)/shard_map/ppermute | solution.py:293
  20.3 6.3 %collective-permute-start.6 = (bf16[512,128]{1,0:T(8,128)(2,1)S(1)}, bf16[512,128]{1,0:T(8,128)(2,1)S(1)}, u32[]{:S(2)}, u32[]{:S(2)}) collective-permute-start(bf16[512,128]{1,0:T(8,128)(2,1)S(1)} %get-tuple-element.25), channel_id=1, source_target_pairs={{0,4},{4,0},{8,12},{12,8},{16,20},{20,16},{24,28},{28,24},{1,5},{5... | collective-permute-start | bytes 393224 | tf_op jit(solution)/shard_map/ppermute | solution.py:293
  22.3 5.0 %collective-permute-start.7 = (bf16[512,128]{1,0:T(8,128)(2,1)S(1)}, bf16[512,128]{1,0:T(8,128)(2,1)S(1)}, u32[]{:S(2)}, u32[]{:S(2)}) collective-permute-start(bf16[512,128]{1,0:T(8,128)(2,1)S(1)} %get-tuple-element.26), channel_id=1, source_target_pairs={{0,8},{4,12},{8,0},{12,4},{16,24},{20,28},{24,16},{28,20},{1,9},{5... | collective-permute-start | bytes 393224 | tf_op jit(solution)/shard_map/ppermute | solution.py:293
  23.4 5.9 %collective-permute-start.8 = (bf16[512,128]{1,0:T(8,128)(2,1)S(1)}, bf16[512,128]{1,0:T(8,128)(2,1)S(1)}, u32[]{:S(2)}, u32[]{:S(2)}) collective-permute-start(bf16[512,128]{1,0:T(8,128)(2,1)S(1)} %shard_map.91), channel_id=1, source_target_pairs={{0,12},{4,8},{8,4},{12,0},{16,28},{20,24},{24,20},{28,16},{1,13},{... | collective-permute-start | bytes 393224 | tf_op jit(solution)/shard_map/ppermute | solution.py:293
